TPU v7x, 128 devices: a whole 4x4x4 slice. The times are simulated.
128 devices in a mesh: dp: 32 (over x, y, core), tensor: 4 (over z).
Axes of the slice: x: 4, y: 4, z: 4, core: 2. Of those that a mesh axis runs over, the one named last changes fastest.
Arguments:
- activations: bfloat16 [65536, 8192], P('dp', 'tensor'), may hold values from -16 to 16
- whitening: bfloat16 [8192, 1024], P('tensor'), may hold values from -8 to 8
- factor: bfloat16 [1024, 1024], P(('dp', 'tensor')), may hold values from -2 to 2
Outputs:
- new_factor: float32 [1024, 1024], P(('dp', 'tensor'))
All inputs are finite; a program needn't handle non-finite values.
Results may differ from a plain program's by a relative error of at most 0.029.
Values may be sent and summed in bfloat16 or wider, within the bound.
A program may use at most 192 MiB of HBM per device.

v0:
```python
import jax
import jax.numpy as jnp
from jax import lax
from jax.sharding import PartitionSpec as P

ridge_shift = 0.1
epsilon = 1e-06


def solve_rows(moment_rows, hadamard):
    lower = jnp.linalg.cholesky(hadamard)
    first = jax.scipy.linalg.solve_triangular(lower, moment_rows.T, lower=True)
    second = jax.scipy.linalg.solve_triangular(lower, first, lower=True, trans=1)
    return second.T


def shards(activations, whitening, factor):
    summed = lax.psum_scatter(
        jnp.dot(activations, whitening, preferred_element_type=jnp.float32).astype(jnp.bfloat16),
        "tensor",
        scatter_dimension=0,
        tiled=True,
    )
    whole_factor = lax.all_gather(factor, ("dp", "tensor"), axis=0, tiled=True)
    projected = jnp.dot(summed, whole_factor, preferred_element_type=jnp.float32)
    squared = (projected * projected).astype(jnp.bfloat16)
    moment_rows = lax.psum_scatter(
        lax.dot_general(
            summed, squared, (((0,), (0,)), ((), ())), preferred_element_type=jnp.float32
        ),
        ("dp", "tensor"),
        scatter_dimension=0,
        tiled=True,
    )
    gram = jnp.dot(whole_factor.T, whole_factor, preferred_element_type=jnp.float32)
    hadamard = gram * gram + ridge_shift * jnp.eye(gram.shape[0], dtype=jnp.float32)
    updated = solve_rows(moment_rows, hadamard)
    column_total = lax.psum(jnp.sum(updated * updated, axis=0), ("dp", "tensor"))
    scale = jnp.sqrt(column_total / whole_factor.shape[0] + epsilon)
    return updated / scale[None, :]


def solution(mesh):
    placed = (P("dp", "tensor"), P("tensor", None), P(("dp", "tensor"), None))
    return jax.shard_map(
        shards, mesh=mesh, in_specs=placed, out_specs=P(("dp", "tensor"), None), check_vma=False
    )
```

profile of v0, /device:TPU:1, one launch (start us, length us, event | category | flops | bytes accessed | tf_op | source)
XLA Modules:
  0.0 901.7 jit_solution(2923321162316526728)
XLA Ops:
  8.1 13.8 %convolution_convert_fusion = bf16[2048,1024]{1,0:T(8,128)(2,1)} fusion(bf16[2048,2048]{1,0:T(8,128)(2,1)} %param.3, bf16[2048,1024]{1,0:T(8,128)(2,1)} %param.4), kind=kOutput, calls=%fused_computation.8 | convolution fusion | flops 8592031744 | bytes 16777216 | tf_op jit(solution)/shard_map/dot_general | solution.py:19
  22.0 77.6 %all-gather.2.cloned.1.call-done = bf16[1024,1024]{1,0:T(8,128)(2,1)} async-done(((bf16[8,1024]{1,0:T(8,128)(2,1)}), bf16[1024,1024]{1,0:T(8,128)(2,1)}) %all-gather.2.cloned.1.call-update) | async-done | bytes 2097168 | tf_op jit(solution)/shard_map/all_gather | solution.py:24
  99.6 4.6 fusion.95
  104.3 2.0 copy-done
  106.2 2.4 multiply_bitcast_fusion
  108.6 5.8 copy.4
  114.4 4.5 add_multiply_fusion
  118.9 2.0 copy-done.1
  120.9 11.7 %cholesky.222 = f32[128,128]{1,0:T(8,128)S(1)} custom-call(f32[128,128]{1,0:T(8,128)S(1)} %cholesky.577), custom_call_target="Cholesky" | custom-call | tf_op jit(solution)/shard_map/jit(cholesky)/cholesky | solution.py:11
  132.6 2.5 cholesky.254
  135.1 9.8 %custom-call.66 = f32[1,128,128]{1,2,0:T(8,128)S(1)} custom-call(f32[1,128,128]{2,1,0:T(8,128)S(1)} %get-tuple-element.44), custom_call_target="InvertDiagBlocksLowerTriangular" | custom-call | tf_op jit(solution)/shard_map/jit(cholesky)/cholesky | solution.py:11
  144.9 2.3 constant_dynamic-update-slice_fusion.50
  147.3 1.5 convolution_subtract_fusion
  148.8 11.8 %cholesky.243 = f32[128,128]{1,0:T(8,128)S(1)} custom-call(f32[128,128]{1,0:T(8,128)S(1)} %cholesky.581), custom_call_target="Cholesky" | custom-call | tf_op jit(solution)/shard_map/jit(cholesky)/cholesky | solution.py:11
  160.7 5.9 fusion.1
  167.3 9.8 %custom-call.67 = f32[1,128,128]{1,2,0:T(8,128)S(1)} custom-call(f32[1,128,128]{2,1,0:T(8,128)S(1)} %get-tuple-element.41), custom_call_target="InvertDiagBlocksLowerTriangular" | custom-call | tf_op jit(solution)/shard_map/jit(cholesky)/cholesky | solution.py:11
  177.1 1.2 convolution_dynamic-update-slice_fusion
  178.3 2.1 convolution_subtract_fusion.1
  180.4 11.7 %cholesky.466 = f32[128,128]{1,0:T(8,128)S(1)} custom-call(f32[128,128]{1,0:T(8,128)S(1)} %cholesky.586), custom_call_target="Cholesky" | custom-call | tf_op jit(solution)/shard_map/jit(cholesky)/cholesky | solution.py:11
  192.8 9.8 %custom-call.68 = f32[1,128,128]{1,2,0:T(8,128)S(1)} custom-call(f32[1,128,128]{2,1,0:T(8,128)S(1)} %get-tuple-element.38), custom_call_target="InvertDiagBlocksLowerTriangular" | custom-call | tf_op jit(solution)/shard_map/jit(cholesky)/cholesky | solution.py:11
  202.6 1.2 convolution_dynamic-update-slice_fusion.1
  203.8 2.5 convolution_subtract_fusion.2
  206.3 11.7 %cholesky.485 = f32[128,128]{1,0:T(8,128)S(1)} custom-call(f32[128,128]{1,0:T(8,128)S(1)} %cholesky.591), custom_call_target="Cholesky" | custom-call | tf_op jit(solution)/shard_map/jit(cholesky)/cholesky | solution.py:11
  218.7 9.8 %custom-call.69 = f32[1,128,128]{1,2,0:T(8,128)S(1)} custom-call(f32[1,128,128]{2,1,0:T(8,128)S(1)} %get-tuple-element.35), custom_call_target="InvertDiagBlocksLowerTriangular" | custom-call | tf_op jit(solution)/shard_map/jit(cholesky)/cholesky | solution.py:11
  228.5 1.1 convolution_dynamic-update-slice_fusion.2
  229.6 2.4 convolution_subtract_fusion.3
  232.0 11.7 %cholesky.504 = f32[128,128]{1,0:T(8,128)S(1)} custom-call(f32[128,128]{1,0:T(8,128)S(1)} %cholesky.596), custom_call_target="Cholesky" | custom-call | tf_op jit(solution)/shard_map/jit(cholesky)/cholesky | solution.py:11
  244.4 10.2 %custom-call.70 = f32[1,128,128]{1,2,0:T(8,128)S(1)} custom-call(f32[1,128,128]{2,1,0:T(8,128)S(1)} %get-tuple-element.32), custom_call_target="InvertDiagBlocksLowerTriangular" | custom-call | tf_op jit(solution)/shard_map/jit(cholesky)/cholesky | solution.py:11
  254.6 1.0 convolution_dynamic-update-slice_fusion.3
  255.6 2.3 convolution_subtract_fusion.4
  257.9 11.7 %cholesky.524 = f32[128,128]{1,0:T(8,128)S(1)} custom-call(f32[128,128]{1,0:T(8,128)S(1)} %cholesky.601), custom_call_target="Cholesky" | custom-call | tf_op jit(solution)/shard_map/jit(cholesky)/cholesky | solution.py:11
  270.2 9.8 %custom-call.71 = f32[1,128,128]{1,2,0:T(8,128)S(1)} custom-call(f32[1,128,128]{2,1,0:T(8,128)S(1)} %get-tuple-element.29), custom_call_target="InvertDiagBlocksLowerTriangular" | custom-call | tf_op jit(solution)/shard_map/jit(cholesky)/cholesky | solution.py:11
  281.0 2.0 convolution_subtract_fusion.5
  283.0 11.9 %cholesky.544 = f32[128,128]{1,0:T(8,128)S(1)} custom-call(f32[128,128]{1,0:T(8,128)S(1)} %cholesky.606), custom_call_target="Cholesky" | custom-call | tf_op jit(solution)/shard_map/jit(cholesky)/cholesky | solution.py:11
  295.5 9.8 %custom-call.72 = f32[1,128,128]{1,2,0:T(8,128)S(1)} custom-call(f32[1,128,128]{2,1,0:T(8,128)S(1)} %get-tuple-element.26), custom_call_target="InvertDiagBlocksLowerTriangular" | custom-call | tf_op jit(solution)/shard_map/jit(cholesky)/cholesky | solution.py:11
  306.2 1.8 convolution_subtract_fusion.6
  308.0 11.7 %cholesky.562 = f32[128,128]{1,0:T(8,128)S(1)} custom-call(f32[128,128]{1,0:T(8,128)S(1)} %convolution_subtract_fusion.6), custom_call_target="Cholesky" | custom-call | tf_op jit(solution)/shard_map/jit(cholesky)/cholesky | solution.py:11
  329.9 4.8 select_select_fusion
  334.7 22.5 %while.1 = (s32[]{:T(128)}, f32[1024,1024]{1,0:T(8,128)}, s32[8,2]{0,1:T(2,128)S(1)}, f32[8,128,128]{2,1,0:T(8,128)S(1)}, s32[]{:T(128)}) while((s32[]{:T(128)}, f32[1024,1024]{1,0:T(8,128)}, s32[8,2]{0,1:T(2,128)S(1)}, f32[8,128,128]{2,1,0:T(8,128)S(1)}, s32[]{:T(128)}) %tuple.56), condition=%wide.while_cond, body=%wide.while_body.sunk | while | flops 2 | bytes 131189 | solution.py:13
  335.3 2.2 bitcast_dynamic-update-slice_fusion.2
  338.1 2.2 bitcast_dynamic-update-slice_fusion.2
  340.9 2.2 bitcast_dynamic-update-slice_fusion.2
  343.8 2.2 bitcast_dynamic-update-slice_fusion.2
  346.6 2.2 bitcast_dynamic-update-slice_fusion.2
  349.4 2.2 bitcast_dynamic-update-slice_fusion.2
  352.2 2.2 bitcast_dynamic-update-slice_fusion.2
  355.0 2.1 bitcast_dynamic-update-slice_fusion.2
  357.2 78.8 %custom-call.73 = f32[8,128,128]{1,2,0:T(8,128)S(1)} custom-call(f32[8,128,128]{2,1,0:T(8,128)S(1)} %get-tuple-element.12), custom_call_target="InvertDiagBlocksLowerTriangular" | custom-call | tf_op jit(solution)/shard_map/jit(_solve_triangular)/triangular_solve | solution.py:13
  436.0 365.3 %reduce-scatter.5.cloned.1.call-done = f32[8,1024]{1,0:T(8,128)} async-done(((f32[1024,1024]{1,0:T(8,128)}), f32[8,1024]{1,0:T(8,128)}) %reduce-scatter.5.cloned.1.call-update) | async-done | bytes 32784 | tf_op jit(solution)/shard_map/reduce_scatter | solution.py:27
  802.1 1.0 convolution_subtract_fusion.16
  803.3 1.1 convolution_subtract_fusion.15
  804.6 1.2 convolution_subtract_fusion.14
  806.0 1.2 convolution_subtract_fusion.13
  807.5 1.4 convolution_subtract_fusion.12
  809.1 1.4 convolution_subtract_fusion.20
  810.6 1.5 convolution_subtract_fusion.19
  812.7 1.0 convolution_subtract_fusion.11
  814.0 1.1 convolution_subtract_fusion.10
  815.3 1.2 convolution_subtract_fusion.9
  816.7 1.2 convolution_subtract_fusion.8
  818.2 1.3 convolution_subtract_fusion.7
  819.7 1.3 convolution_subtract_fusion.18
  821.3 1.4 convolution_subtract_fusion.17
  823.0 70.4 %psum.7 = f32[1024]{0:T(1024)S(1)} all-reduce(f32[1024]{0:T(1024)S(1)} %multiply_reduce_fusion), channel_id=1, replica_groups=mesh['dp'=32,'tensor'=4] {'dp','tensor'}, use_global_device_ids=true, to_apply=%region_19.20 | all-reduce | flops 1024 | bytes 8192 | tf_op jit(solution)/shard_map/psum | solution.py:38
  (95 shorter events, 21.3 us)
Async XLA Ops:
  7.4 92.3 %all-gather.2.cloned.1.call-start = ((), (), s32[]{:S(2)}) async-start(), calls=%async_computation.2 | async-start | bytes 2113536 | tf_op jit(solution)/shard_map/all_gather | solution.py:24
  8.1 152.6 %reduce-scatter.3.cloned.1.call-start = ((), (), s32[]{:S(2)}) async-start(), calls=%async_computation.3 | async-start | bytes 5242880 | tf_op jit(solution)/shard_map/reduce_scatter | solution.py:18
  21.9 779.3 %reduce-scatter.5.cloned.1.call-start = ((), (), s32[]{:S(2)}) async-start(), calls=%async_computation.4 | async-start | bytes 4227072 | tf_op jit(solution)/shard_map/reduce_scatter | solution.py:27
  104.2 2.0 copy-start
  118.9 2.0 copy-start.1
  120.8 39.9 %copy-start.2 = (bf16[1024,1024]{1,0:T(8,128)(2,1)S(1)}, bf16[1024,1024]{1,0:T(8,128)(2,1)}, u32[]{:S(2)}) copy-start(bf16[1024,1024]{1,0:T(8,128)(2,1)} %all-gather.2.cloned.1.call-done) | copy-start | bytes 6291460
Sparse Core Ops, SparseCore 0:
  11.2 88.4 all-gather.1
  166.7 634.4 reduce-scatter.4
Sparse Core Ops, SparseCore 1:
  22.0 50.3 reduce-scatter.2
where the time goes:
time: 908 us; the launch traced here: 902 us
  waiting for transfers between devices  444 us (49%)
  other arithmetic  263 us (29%)
  blocking collectives  70.4 us (8%)
  matrix products  68.9 us (8%)
  local copies, waits for them, and re-layouts  34.8 us (4%)
  between operations  20.4 us (2%)
    reduce_scatter x1, waiting for transfers between devices, shards(): lax.psum_scatter(lax.dot_general(summed, squared, (((0,), (0,)), ((), ())...  365 us
    another operation x30, other arithmetic, solve_rows(): lower = jnp.linalg.cholesky(hadamard)  172 us
    another operation x3, other arithmetic, solve_rows(): jax.scipy.linalg.solve_triangular(lower, first, lower=True, trans=1)  83.6 us
    all_gather x1, waiting for transfers between devices, shards(): whole_factor = lax.all_gather(factor, ('dp', 'tensor'), axis=0, tiled=True)  77.6 us
    psum x1, blocking collectives, shards(): lax.psum(jnp.sum(updated * updated, axis=0), ('dp', 'tensor'))  70.4 us
    another operation x14, matrix products, solve_rows(): lower = jnp.linalg.cholesky(hadamard)  23.3 us
    another operation x24, local copies, waits for them, and re-layouts  22.3 us
  transfers between devices with their start and end apart: 3, of which 2 were waited for; matrix products, arithmetic and copies ran while one was open for 37% of the time, Pallas kernels for 0%

commit v1 on v0

v1 whole, which is shorter than its diff:
```python
import jax, jax.numpy as jnp
from jax import lax
from jax.sharding import PartitionSpec as P
from jax.experimental import pallas as pl
from jax.experimental.pallas import tpu as pltpu

F32, BF16 = jnp.float32, jnp.bfloat16
HI = lax.Precision.HIGHEST

def over_lanes(x, j):
    return jnp.broadcast_to(x[:, j:j + 1], (8, 128))

def over_sublanes(x, j):
    return jnp.broadcast_to(x[j:j + 1, :], (8, 128))

def invert_block(rows):
    lane = lax.broadcasted_iota(jnp.int32, (8, 128), 1)
    sub = lax.broadcasted_iota(jnp.int32, (8, 128), 0)
    count = len(rows)
    for s in range(count):
        inside = (lane >= 8 * s) & (lane < 8 * s + 8)
        panel = rows[s]
        cols = [over_lanes(panel, 8 * s + j) for j in range(8)]
        z = jnp.where(inside, jnp.where(lane - 8 * s == sub, 1.0, 0.0), panel)
        for m in range(4):
            a, b = 2 * m, 2 * m + 1
            ea, eb = cols[a], cols[b]
            g00, g10 = over_sublanes(ea, a), over_sublanes(ea, b)
            g01, g11 = over_sublanes(eb, a), over_sublanes(eb, b)
            r = 1.0 / (g00 * g11 - g01 * g10)
            q00, q01, q10, q11 = g11 * r, -g01 * r, -g10 * r, g00 * r
            fa = -(ea * q00 + eb * q10)
            fb = -(ea * q01 + eb * q11)
            fa = jnp.where(sub == a, q00, jnp.where(sub == b, q10, fa))
            fb = jnp.where(sub == a, q01, jnp.where(sub == b, q11, fb))
            pair = (sub == a) | (sub == b)

            def step(v):
                return (jnp.where(pair, 0.0, v) + fa * over_sublanes(v, a)) + fb * over_sublanes(v, b)

            z = step(z)
            for c in range(b + 1, 8):
                cols[c] = step(cols[c])
        trow = [over_sublanes(z, j) for j in range(8)]
        for i in range(count):
            if i != s:
                v = rows[i]
                p = [over_lanes(v, 8 * s + j) * trow[j] for j in range(8)]
                total = ((p[0] + p[1]) + (p[2] + p[3])) + ((p[4] + p[5]) + (p[6] + p[7]))
                rows[i] = jnp.where(inside, 0.0, v) - total
        rows[s] = z
    return rows

def split(x):
    one = x.astype(BF16)
    rest = x - one.astype(F32)
    two = rest.astype(BF16)
    three = (rest - two.astype(F32)).astype(BF16)
    return one, two, three

def inverse_kernel(f_ref, a_ref, inv_ref, left, right):
    n = 1024
    for j in range(4):
        g = lax.dot_general(f_ref[:, 256 * j:256 * j + 256], f_ref[...], (((0,), (0,)), ((), ())), preferred_element_type=F32)
        row = lax.broadcasted_iota(jnp.int32, (256, n), 0) + 256 * j
        col = lax.broadcasted_iota(jnp.int32, (256, n), 1)
        h = g * g + jnp.where(row == col, 0.1, 0.0)
        a_ref[256 * j:256 * j + 256, :] = h
        inv_ref[256 * j:256 * j + 256, :] = h

    def step(k, carry):
        k0 = pl.multiple_of(k * 128, 128)
        block = [inv_ref[pl.ds(pl.multiple_of(k0 + 8 * i, 8), 8), pl.ds(k0, 128)] for i in range(16)]
        p = jnp.concatenate(invert_block(block), axis=0)
        panel = inv_ref[pl.ds(k0, 128), :]
        t = jnp.dot(p, panel, precision=HI, preferred_element_type=F32)
        inv_ref[pl.ds(k0, 128), :] = t
        inv_ref[pl.ds(k0, 128), pl.ds(k0, 128)] = p
        t1, t2, t3 = split(inv_ref[pl.ds(k0, 128), :])
        for i, piece in enumerate((t1, t2, t1, t3, t2, t1)):
            right[128 * i:128 * i + 128, :] = piece
        row = lax.broadcasted_iota(jnp.int32, (n, 128), 0)
        own = (row >= k0) & (row < k0 + 128)
        c = jnp.where(own, 0.0, inv_ref[:, pl.ds(k0, 128)])
        c1, c2, c3 = split(c)
        for i, piece in enumerate((c1, c1, c2, c1, c2, c3)):
            left[:, 128 * i:128 * i + 128] = piece
        inv_ref[:, pl.ds(k0, 128)] = jnp.where(own, inv_ref[:, pl.ds(k0, 128)], 0.0)
        for r in range(4):
            rows = slice(256 * r, 256 * r + 256)
            inv_ref[rows, :] -= jnp.dot(left[rows, :], right[...], preferred_element_type=F32)
        return carry

    lax.fori_loop(0, n // 128, step, 0)

def inverse(f):
    n = 1024
    return pl.pallas_call(
        inverse_kernel,
        out_shape=(jax.ShapeDtypeStruct((n, n), F32), jax.ShapeDtypeStruct((n, n), F32)),
        in_specs=[pl.BlockSpec(memory_space=pltpu.VMEM)],
        out_specs=(pl.BlockSpec(memory_space=pltpu.VMEM), pl.BlockSpec(memory_space=pltpu.VMEM)),
        scratch_shapes=[pltpu.VMEM((n, 768), BF16), pltpu.VMEM((768, n), BF16)],
        compiler_params=pltpu.CompilerParams(vmem_limit_bytes=40 * 2**20),
    )(f)

MESH = pl.DeviceIdType.MESH

def place():
    dp, z = lax.axis_index("dp"), lax.axis_index("tensor")
    return dp // 8, (dp // 2) % 4, dp % 2, z

def peer(x, y, c, z, d):
    px = lax.rem(x + d // 16, 4)
    py = lax.rem(y + lax.rem(d // 4, 4), 4)
    pz = lax.rem(z + lax.rem(d, 4), 4)
    return (px, py, pz), ((px * 4 + py) * 2 + c, pz)

def greet(x, y, c, z):
    barrier = pltpu.get_barrier_semaphore()

    def one(d, carry):
        _, device = peer(x, y, c, z, d)
        pl.semaphore_signal(barrier, inc=1, device_id=device, device_id_type=MESH)
        return carry

    lax.fori_loop(1, 64, one, 0)
    pl.semaphore_signal(barrier, inc=1, device_id=((x * 4 + y) * 2 + 1 - c, z), device_id_type=MESH)
    return barrier

def gather_kernel(f_ref, out_ref, send, recv, core_send, core_recv, own):
    x, y, c, z = place()
    barrier = greet(x, y, c, z)
    home = out_ref.at[x * 4 + y, c, z]
    copy_in = pltpu.make_async_copy(f_ref, home, own)
    copy_in.start()
    pl.semaphore_wait(barrier, 64)

    def put(d):
        _, device = peer(x, y, c, z, d)
        return pltpu.make_async_remote_copy(
            src_ref=f_ref, dst_ref=home, send_sem=send.at[d], recv_sem=recv.at[d], device_id=device, device_id_type=MESH)

    def start(d, carry):
        put(d).start()
        return carry

    def finish(d, carry):
        put(d).wait()
        return carry

    lax.fori_loop(1, 64, start, 0)
    copy_in.wait()
    lax.fori_loop(1, 64, finish, 0)
    half = out_ref.at[:, c]
    across = pltpu.make_async_remote_copy(
        src_ref=half, dst_ref=half, send_sem=core_send, recv_sem=core_recv,
        device_id=((x * 4 + y) * 2 + 1 - c, z), device_id_type=MESH)
    across.start()
    across.wait()

def gather(f):
    return pl.pallas_call(
        gather_kernel,
        out_shape=jax.ShapeDtypeStruct((16, 2, 4, 8, 1024), BF16),
        in_specs=[pl.BlockSpec(memory_space=pltpu.VMEM)],
        out_specs=pl.BlockSpec(memory_space=pltpu.VMEM),
        scratch_shapes=[pltpu.SemaphoreType.DMA((64,)), pltpu.SemaphoreType.DMA((64,)),
                        pltpu.SemaphoreType.DMA, pltpu.SemaphoreType.DMA, pltpu.SemaphoreType.DMA],
        compiler_params=pltpu.CompilerParams(collective_id=0, has_side_effects=True),
    )(f)

def finish_kernel(m_ref, inv_ref, out_ref, core_out, core_in, mine, parts, norm_out, norm_in,
                  send, recv, core_send, core_recv, nsend, nrecv, ncore_send, ncore_recv):
    x, y, c, z = place()
    barrier = greet(x, y, c, z)
    partner = ((x * 4 + y) * 2 + 1 - c, z)

    def cast(i, carry):
        core_out[i] = m_ref[i, 1 - c].astype(BF16)
        return carry

    lax.fori_loop(0, 16, cast, 0)
    pl.semaphore_wait(barrier, 64)
    across = pltpu.make_async_remote_copy(
        src_ref=core_out, dst_ref=core_in, send_sem=core_send, recv_sem=core_recv, device_id=partner, device_id_type=MESH)
    across.start()
    across.wait()

    def add(i, carry):
        mine[i] = (m_ref[i, c] + core_in[i].astype(F32)).astype(BF16)
        return carry

    lax.fori_loop(0, 16, add, 0)

    def put(d):
        (px, py, pz), device = peer(x, y, c, z, d)
        return pltpu.make_async_remote_copy(
            src_ref=mine.at[px * 4 + py, pz], dst_ref=parts.at[d], send_sem=send.at[d], recv_sem=recv.at[d],
            device_id=device, device_id_type=MESH)

    def start(d, carry):
        put(d).start()
        return carry

    def finish(d, total):
        put(d).wait()
        return total + parts[d].astype(F32)

    lax.fori_loop(1, 64, start, 0)
    home = x * 4 + y
    total = m_ref[home, c, z] + core_in[home, z].astype(F32)
    total = lax.fori_loop(1, 64, finish, total)
    updated = jnp.dot(total, inv_ref[...], precision=HI, preferred_element_type=F32)
    squares = jnp.sum(updated * updated, axis=0, keepdims=True)
    for j in range(8):
        norm_out[0, j:j + 1, :] = squares[:, 128 * j:128 * j + 128]
    ncore = pltpu.make_async_remote_copy(
        src_ref=norm_out.at[0], dst_ref=norm_in.at[0], send_sem=ncore_send, recv_sem=ncore_recv, device_id=partner, device_id_type=MESH)
    ncore.start()
    ncore.wait()
    norm_out[1] = norm_out[0] + norm_in[0]

    def nput(d):
        _, device = peer(x, y, c, z, d)
        return pltpu.make_async_remote_copy(
            src_ref=norm_out.at[1], dst_ref=norm_in.at[d], send_sem=nsend.at[d], recv_sem=nrecv.at[d],
            device_id=device, device_id_type=MESH)

    def nstart(d, carry):
        nput(d).start()
        return carry

    def nfinish(d, total):
        nput(d).wait()
        return total + norm_in[d]

    lax.fori_loop(1, 64, nstart, 0)
    norm = lax.fori_loop(1, 64, nfinish, norm_out[1])
    inverse_scale = 1.0 / jnp.sqrt(norm * (1.0 / 1024) + 1e-6)
    for j in range(8):
        out_ref[:, 128 * j:128 * j + 128] = updated[:, 128 * j:128 * j + 128] * inverse_scale[j:j + 1, :]

def finish(m, inv):
    return pl.pallas_call(
        finish_kernel,
        out_shape=jax.ShapeDtypeStruct((8, 1024), F32),
        in_specs=[pl.BlockSpec(memory_space=pltpu.VMEM)] * 2,
        out_specs=pl.BlockSpec(memory_space=pltpu.VMEM),
        scratch_shapes=[
            pltpu.VMEM((16, 4, 8, 1024), BF16), pltpu.VMEM((16, 4, 8, 1024), BF16), pltpu.VMEM((16, 4, 8, 1024), BF16),
            pltpu.VMEM((64, 8, 1024), BF16), pltpu.VMEM((2, 8, 128), F32), pltpu.VMEM((64, 8, 128), F32),
            pltpu.SemaphoreType.DMA((64,)), pltpu.SemaphoreType.DMA((64,)), pltpu.SemaphoreType.DMA, pltpu.SemaphoreType.DMA,
            pltpu.SemaphoreType.DMA((64,)), pltpu.SemaphoreType.DMA((64,)), pltpu.SemaphoreType.DMA, pltpu.SemaphoreType.DMA],
        compiler_params=pltpu.CompilerParams(collective_id=1, has_side_effects=True, vmem_limit_bytes=40 * 2**20),
    )(m, inv)


def shards(activations, whitening, factor):
    partial = jnp.dot(activations, whitening, preferred_element_type=F32).astype(BF16)
    summed = lax.psum_scatter(partial, "tensor", scatter_dimension=0, tiled=True)
    whole_factor = gather(factor).reshape(1024, 1024)
    hadamard, inv = inverse(whole_factor)
    projected = jnp.dot(summed, whole_factor, preferred_element_type=F32)
    squared = (projected * projected).astype(BF16)
    moment = lax.dot_general(summed, squared, (((0,), (0,)), ((), ())), preferred_element_type=F32)
    return finish(moment.reshape(16, 2, 4, 8, 1024), inv)


def solution(mesh):
    placed = (P("dp", "tensor"), P("tensor", None), P(("dp", "tensor"), None))
    return jax.shard_map(
        shards, mesh=mesh, in_specs=placed, out_specs=P(("dp", "tensor"), None), check_vma=False
    )
```

time: 908 us -> 186 us (0.20)
  waiting for transfers between devices: 444 us -> 0.02 us
  other arithmetic: 263 us -> 0 us
  Pallas kernels: 0 us -> 143 us
  blocking collectives: 70.4 us -> 0 us
  matrix products: 68.9 us -> 20.3 us
  local copies, waits for them, and re-layouts: 34.8 us -> 8.55 us
    reduce_scatter x2 -> x1, waiting for transfers between devices: 365 us -> 0.01 us  [shards(): lax.psum_scatter(partial, 'tensor', scatter_dimension=0, tiled=True)]
    another operation x33 -> x0, other arithmetic: 256 us -> none  [the longest x30 172 us: solve_rows(): lower = jnp.linalg.cholesky(hadamard)]
    pallas_call x0 -> x3, Pallas kernels: none -> 143 us  [the longest x1 69.9 us: inverse(): pl.pallas_call(inverse_kernel, out_shape=(jax.ShapeDtypeStruct((n, n), F3...]
    all_gather x1 -> x0, waiting for transfers between devices: 77.6 us -> none  [shards(): whole_factor = lax.all_gather(factor, ('dp', 'tensor'), axis=0, tiled=True)]
    psum x1 -> x0, blocking collectives: 70.4 us -> none  [shards(): lax.psum(jnp.sum(updated * updated, axis=0), ('dp', 'tensor'))]
    another operation x44 -> x0, matrix products: 44.7 us -> none  [the longest x14 23.3 us: solve_rows(): lower = jnp.linalg.cholesky(hadamard)]
    another operation x37 -> x0, local copies, waits for them, and re-layouts: 24.9 us -> none
    dot_general x2 -> x1, matrix products: 18.4 us -> 13.8 us  [shards(): jnp.dot(activations, whitening, preferred_element_type=F32).astype(BF16)]
  transfers between devices with their start and end apart: 3 -> 1, of which waited for: 2 -> 0; matrix products, arithmetic and copies ran while one was open for 37% -> 0% of each run, Pallas kernels for 0% -> 55%
where the time goes in v1:
time: 186 us
  Pallas kernels  143 us (77%)
  matrix products  20.3 us (11%)
  between operations  13.4 us (7%)
  local copies, waits for them, and re-layouts  8.55 us (5%)
    pallas_call x1, Pallas kernels, inverse(): pl.pallas_call(inverse_kernel, out_shape=(jax.ShapeDtypeStruct((n, n), F3...  69.9 us
    pallas_call x1, Pallas kernels, finish(): pl.pallas_call(finish_kernel, out_shape=jax.ShapeDtypeStruct((8, 1024), F...  41 us
    pallas_call x1, Pallas kernels, gather(): pl.pallas_call(gather_kernel, out_shape=jax.ShapeDtypeStruct((16, 2, 4, 8...  32.4 us
    dot_general x1, matrix products, shards(): jnp.dot(activations, whitening, preferred_element_type=F32).astype(BF16)  13.8 us
    unnamed x9, local copies, waits for them, and re-layouts  8.55 us
    dot_general x1, matrix products, shards(): lax.dot_general(summed, squared, (((0,), (0,)), ((), ())), preferred_elem...  6.51 us
  transfers between devices with their start and end apart: 1, of which 0 were waited for; matrix products, arithmetic and copies ran while one was open for 0% of the time, Pallas kernels for 55%

profile of v1, /device:TPU:1, one launch (start us, length us, event | category | flops | bytes accessed | tf_op | source)
XLA Modules:
  0.0 185.6 jit_solution(9489070992697445508)
XLA Ops:
  6.5 0.0 reduce-scatter.2.cloned.1.call-start
  6.5 13.8 %convolution_convert_fusion = bf16[2048,1024]{1,0:T(8,128)(2,1)} fusion(bf16[2048,2048]{1,0:T(8,128)(2,1)} %param.3, bf16[2048,1024]{1,0:T(8,128)(2,1)} %param.4), kind=kOutput, calls=%fused_computation | convolution fusion | flops 8592031744 | bytes 16777216 | tf_op jit(solution)/shard_map/dot_general | solution.py:260
  20.3 0.0 reduce-scatter.2.cloned.1.call-update
  20.3 32.4 %shard_map.37 = bf16[16,2,4,8,1024]{4,3,2,1,0:T(8,128)(2,1)} custom-call(bf16[8,1024]{1,0:T(8,128)(2,1)} %f_ref.1), custom_call_target="tpu_custom_call" | custom-call | tf_op jit(solution)/shard_map/pallas_call | solution.py:163
  52.7 0.0 copy-start
  52.8 1.6 copy-done
  54.3 69.9 %shard_map.38 = (f32[1024,1024]{1,0:T(8,128)}, f32[1024,1024]{1,0:T(8,128)S(1)}) custom-call(bf16[1024,1024]{1,0:T(8,128)(2,1)S(1)} %bitcast.8), custom_call_target="tpu_custom_call" | custom-call | tf_op jit(solution)/shard_map/pallas_call | solution.py:98
  124.3 0.0 copy-start.1
  124.3 2.0 %copy-done.1 = f32[1024,1024]{1,0:T(8,128)} copy-done((f32[1024,1024]{1,0:T(8,128)}, f32[1024,1024]{1,0:T(8,128)S(1)}, u32[]{:S(2)}) %copy-start.1) | copy-done | bytes 4194328
  126.2 0.0 reduce-scatter.2.cloned.1.call-done
  126.2 6.5 %fusion = f32[1024,1024]{1,0:T(8,128)} fusion(bf16[512,1024]{1,0:T(8,128)(2,1)} %reduce-scatter.2.cloned.1.call-done, bf16[1024,1024]{1,0:T(8,128)(2,1)} %bitcast.7), kind=kOutput, calls=%fused_computation.2 | convolution fusion | flops 2148532224 | bytes 7340032 | tf_op jit(solution)/shard_map/dot_general | solution.py:266
  132.8 0.0 copy-start.2
  132.8 2.2 %copy-done.2 = f32[1024,1024]{1,0:T(8,128)S(1)} copy-done((f32[1024,1024]{1,0:T(8,128)S(1)}, f32[1024,1024]{1,0:T(8,128)}, u32[]{:S(2)}) %copy-start.2) | copy-done | bytes 4194328
  134.9 0.0 copy-start.3
  134.9 2.2 %copy-done.3 = f32[1024,1024]{1,0:T(8,128)S(1)} copy-done((f32[1024,1024]{1,0:T(8,128)S(1)}, f32[1024,1024]{1,0:T(8,128)}, u32[]{:S(2)}) %copy-start.3) | copy-done | bytes 4194328
  137.1 41.0 %shard_map.39 = f32[8,1024]{1,0:T(8,128)S(1)} custom-call(f32[16,2,4,8,1024]{4,3,2,1,0:T(8,128)S(1)} %bitcast.9, f32[1024,1024]{1,0:T(8,128)S(1)} %copy-done.2), custom_call_target="tpu_custom_call" | custom-call | tf_op jit(solution)/shard_map/pallas_call | solution.py:245
  178.1 0.6 copy.5
Async XLA Ops:
  6.5 119.7 %reduce-scatter.2.cloned.1.call-start = ((), (), s32[]{:S(2)}) async-start(), calls=%async_computation.1 | async-start | bytes 5242880 | tf_op jit(solution)/shard_map/reduce_scatter | solution.py:261
  52.7 1.6 copy-start
  124.3 2.0 %copy-start.1 = (f32[1024,1024]{1,0:T(8,128)}, f32[1024,1024]{1,0:T(8,128)S(1)}, u32[]{:S(2)}) copy-start(f32[1024,1024]{1,0:T(8,128)S(1)} %get-tuple-element.6.inv_ref) | copy-start | bytes 12582916
  132.8 2.2 %copy-start.2 = (f32[1024,1024]{1,0:T(8,128)S(1)}, f32[1024,1024]{1,0:T(8,128)}, u32[]{:S(2)}) copy-start(f32[1024,1024]{1,0:T(8,128)} %copy-done.1) | copy-start | bytes 12582916
  134.9 2.2 %copy-start.3 = (f32[1024,1024]{1,0:T(8,128)S(1)}, f32[1024,1024]{1,0:T(8,128)}, u32[]{:S(2)}) copy-start(f32[1024,1024]{1,0:T(8,128)} %fusion) | copy-start | bytes 12582916
Sparse Core Ops, SparseCore 0:
  20.4 59.7 reduce-scatter.1

commit v2 on v0

v2 whole, which is shorter than its diff:
```python
import jax, jax.numpy as jnp
from jax import lax
from jax.sharding import PartitionSpec as P
from jax.experimental import pallas as pl
from jax.experimental.pallas import tpu as pltpu

F32, BF16 = jnp.float32, jnp.bfloat16
HI = lax.Precision.HIGHEST

def over_lanes(x, j):
    return jnp.broadcast_to(x[:, j:j + 1], (8, 128))

def over_sublanes(x, j):
    return jnp.broadcast_to(x[j:j + 1, :], (8, 128))

def tree(p):
    while len(p) > 1:
        p = [p[i] + p[i + 1] for i in range(0, len(p), 2)]
    return p[0]

def eliminate(rows, cols, first, s, lane, sub):
    base = first + 8 * s
    more = s + 1 < len(rows)
    inside = (lane >= base) & (lane < base + 8)
    panel = rows[s]
    if cols is None:
        cols = [over_lanes(panel, base + j) for j in range(8)]
    cols = list(cols)
    z = jnp.where(inside, jnp.where(lane - base == sub, 1.0, 0.0), panel)
    ahead = [over_lanes(panel, base + 8 + j) for j in range(8)] if more else []
    for m in range(4):
        a, b = 2 * m, 2 * m + 1
        ea, eb = cols[a], cols[b]
        g00, g10 = over_sublanes(ea, a), over_sublanes(ea, b)
        g01, g11 = over_sublanes(eb, a), over_sublanes(eb, b)
        r = 1.0 / (g00 * g11 - g01 * g10)
        q00, q01, q10, q11 = g11 * r, -(g01 * r), -(g10 * r), g00 * r
        fa = -(ea * q00 + eb * q10)
        fb = -(ea * q01 + eb * q11)
        fa = jnp.where(sub == a, q00, jnp.where(sub == b, q10, fa))
        fb = jnp.where(sub == a, q01, jnp.where(sub == b, q11, fb))
        pair = (sub == a) | (sub == b)

        def step(v):
            return (jnp.where(pair, 0.0, v) + fa * over_sublanes(v, a)) + fb * over_sublanes(v, b)

        for c in range(b + 1, 8):
            cols[c] = step(cols[c])
        z = step(z)
        ahead = [step(v) for v in ahead]
    following = None
    trow = [over_sublanes(z, j) for j in range(8)]
    for i in list(range(s + 1, len(rows))) + list(range(s)):
        v = rows[i]
        spread = [over_lanes(v, base + j) for j in range(8)]
        if i == s + 1:
            following = [
                over_lanes(v, base + 8 + j) - tree([spread[m] * over_sublanes(ahead[j], m) for m in range(8)])
                for j in range(8)]
        rows[i] = jnp.where(inside, 0.0, v) - tree([spread[j] * trow[j] for j in range(8)])
    rows[s] = z
    return following

def invert_block(rows, size, fill):
    lane = lax.broadcasted_iota(jnp.int32, (8, 128), 1)
    sub = lax.broadcasted_iota(jnp.int32, (8, 128), 0)
    each = size // 8
    groups = 128 // size
    zero = [jnp.zeros((8, 128), F32)]
    for g in range(groups):
        own = rows[each * g:each * g + each]
        cols = None
        for s in range(each):
            cols = eliminate(own, cols, size * g, s, lane, sub)
            fill()
        rows[each * g:each * g + each] = own
        inside = (lane >= size * g) & (lane < size * g + size)
        t = jnp.concatenate(zero * (each * g) + own + zero * (16 - each * g - each), axis=0)
        for o in [(g + e) % groups for e in range(1, groups)]:
            c = jnp.concatenate([jnp.where(inside, rows[i], 0.0) for i in range(each * o, each * o + each)], axis=0)
            u = jnp.dot(c, t, precision=HI, preferred_element_type=F32)
            for n in range(each):
                i = each * o + n
                rows[i] = jnp.where(inside, 0.0, rows[i]) - u[8 * n:8 * n + 8]
    return rows

TERMS = ((0, 0), (0, 1), (1, 0), (0, 2), (1, 1), (2, 0))
SIZE = 64
N = 1024

def split(x):
    one = x.astype(BF16)
    rest = x - one.astype(F32)
    two = rest.astype(BF16)
    three = (rest - two.astype(F32)).astype(BF16)
    return one, two, three

def hadamard_block(f_ref, i, rows, j, cols):
    g = lax.dot_general(f_ref[:, i:i + rows], f_ref[:, j:j + cols], (((0,), (0,)), ((), ())), preferred_element_type=F32)
    row = lax.broadcasted_iota(jnp.int32, (rows, cols), 0) + i
    col = lax.broadcasted_iota(jnp.int32, (rows, cols), 1) + j
    return g * g + jnp.where(row == col, 0.1, 0.0)

def invert(f_ref, inv_ref, left, right, pivot):
    def run(todo, rate):
        def fill():
            for _ in range(rate):
                if todo:
                    todo.pop(0)()
        return fill

    def fill_rows(j):
        def go():
            inv_ref[128 * j:128 * j + 128, :] = hadamard_block(f_ref, 128 * j, 128, 0, N)
        return go

    d = hadamard_block(f_ref, 0, 128, 0, 128)
    todo = [fill_rows(j) for j in range(8)]
    first = invert_block([d[8 * i:8 * i + 8] for i in range(16)], SIZE, run(todo, 1))
    pivot[...] = jnp.concatenate(first, axis=0)

    def work(k0):
        p = pivot[...]
        row = lax.broadcasted_iota(jnp.int32, (N, 128), 0)
        col = lax.broadcasted_iota(jnp.int32, (128, 256), 1)
        own = (row >= k0) & (row < k0 + 128)
        pp = jnp.concatenate([p, p], axis=1)

        def panel(j):
            def go():
                cols = slice(256 * j, 256 * j + 256)
                t = jnp.dot(p, inv_ref[pl.ds(k0, 128), cols], precision=HI, preferred_element_type=F32)
                at = col + 256 * j
                t = jnp.where((at >= k0) & (at < k0 + 128), pp, t)
                inv_ref[pl.ds(k0, 128), cols] = t
                tt = split(t)
                for i, (a, b) in enumerate(TERMS):
                    right[128 * i:128 * i + 128, cols] = tt[b]
            return go

        def column():
            old = inv_ref[:, pl.ds(k0, 128)]
            cc = split(jnp.where(own, 0.0, old))
            for i, (a, b) in enumerate(TERMS):
                left[:, 128 * i:128 * i + 128] = cc[a]
            inv_ref[:, pl.ds(k0, 128)] = jnp.where(own, old, 0.0)

        def update(r, c):
            def go():
                rows, cols = slice(128 * r, 128 * r + 128), slice(512 * c, 512 * c + 512)
                inv_ref[rows, cols] -= jnp.dot(left[rows, :], right[:, cols], preferred_element_type=F32)
            return go

        return [column] + [panel(j) for j in range(4)] + [update(r, c) for r in range(8) for c in range(2)]

    def step(k, carry):
        k0 = pl.multiple_of(k * 128, 128)
        n0 = pl.multiple_of(k * 128 + 128, 128)
        p = pivot[...]
        tn = jnp.dot(p, inv_ref[pl.ds(k0, 128), pl.ds(n0, 128)], precision=HI, preferred_element_type=F32)
        d = inv_ref[pl.ds(n0, 128), pl.ds(n0, 128)] - jnp.dot(
            inv_ref[pl.ds(n0, 128), pl.ds(k0, 128)], tn, precision=HI, preferred_element_type=F32)
        todo = work(k0)
        nxt = invert_block([d[8 * i:8 * i + 8] for i in range(16)], SIZE, run(todo, 2))
        while todo:
            todo.pop(0)()
        pivot[...] = jnp.concatenate(nxt, axis=0)
        return carry

    lax.fori_loop(0, N // 128 - 1, step, 0)
    for go in work(N - 128):
        go()


MESH = pl.DeviceIdType.MESH
OFFSETS = [(a, b, e) for a in range(4) for b in range(4) for e in range(4) if a + b + e > 0]


def ring(i):
    return [i] + [jnp.where(i + s >= 4, i + s - 4, i + s) for s in (1, 2, 3)]


class Map:
    def __init__(self):
        dp, z = lax.axis_index("dp"), lax.axis_index("tensor")
        x, y, self.c = dp // 8, (dp // 2) % 4, dp % 2
        xs, ys, self.zs = ring(x), ring(y), ring(z)
        self.pos = {o: (xs[o[0]] * 4 + ys[o[1]], self.zs[o[2]]) for o in OFFSETS}
        self.xy, self.z = x * 4 + y, z
        self.partner = (self.xy * 2 + 1 - self.c, z)

    def device(self, o):
        xy, z = self.pos[o]
        return (xy * 2 + self.c, z)


def greet(m):
    barrier = pltpu.get_barrier_semaphore()
    for o in OFFSETS:
        pl.semaphore_signal(barrier, inc=1, device_id=m.device(o), device_id_type=MESH)
    pl.semaphore_signal(barrier, inc=1, device_id=m.partner, device_id_type=MESH)
    return barrier


def remote(src, dst, send, recv, device):
    return pltpu.make_async_remote_copy(
        src_ref=src, dst_ref=dst, send_sem=send, recv_sem=recv, device_id=device, device_id_type=MESH)


def all_of(ref, sem):
    return pltpu.make_async_copy(ref, ref, sem)


def whole_kernel(act_ref, wh_ref, f_ref, out_ref,
                 act, wh, part, far, near, f5, factor, inv, left, right, pivot, summed, squared, moment,
                 core_out, core_in, mine, parts, norm_out, norm_in,
                 act_sem, wh_sem, f_send, f_recv, a_send, a_recv, n_send, n_recv, pair_send, pair_recv, far_send, far_recv, near_send, near_recv):
    m = Map()
    c, z = m.c, m.z
    barrier = greet(m)
    order = (m.zs[2], m.zs[1], m.zs[3], z)
    for r in range(4):
        rows = pl.ds(pl.multiple_of(order[r] * 512, 512), 512)
        pltpu.make_async_copy(act_ref.at[rows, :], act.at[r], act_sem.at[r]).start()
        if r == 0:
            pltpu.make_async_copy(wh_ref, wh, wh_sem).start()
    f5[m.xy, c, z] = f_ref[...]
    pl.semaphore_wait(barrier, 64)

    home = f5.at[m.xy, c, z]
    for o in OFFSETS:
        remote(f_ref, home, f_send, f_recv, m.device(o)).start()

    up, down = m.device((0, 0, 1)), m.device((0, 0, 3))
    far_up = remote(part.at[0, pl.ds(0, 256)], far.at[0], far_send.at[0], far_recv.at[0], up)
    far_down = remote(part.at[0, pl.ds(256, 256)], far.at[1], far_send.at[1], far_recv.at[1], down)
    near_up = remote(part.at[1], near.at[0], near_send.at[0], near_recv.at[0], up)
    near_down = remote(part.at[2], near.at[1], near_send.at[1], near_recv.at[1], down)
    pltpu.make_async_copy(wh_ref, wh, wh_sem).wait()
    for r in range(4):
        rows = pl.ds(pl.multiple_of(order[r] * 512, 512), 512)
        pltpu.make_async_copy(act_ref.at[rows, :], act.at[r], act_sem.at[r]).wait()

        def tile(i, carry, r=r):
            cols = pl.ds(pl.multiple_of(i * 256, 256), 256)
            part[r, :, cols] = jnp.dot(act[r], wh[:, cols], preferred_element_type=F32).astype(BF16)
            return carry

        lax.fori_loop(0, 4, tile, 0)
        if r == 0:
            far_up.start()
            far_down.start()

    all_of(parts, f_recv).wait()
    pair = remote(f5.at[:, c], f5.at[:, c], pair_send.at[0], pair_recv.at[0], m.partner)
    pair.start()

    far_up.wait_recv()

    def add_up(i, carry):
        rows = pl.ds(pl.multiple_of(i * 32, 32), 32)
        part[1, rows, :] = (part[1, rows, :].astype(F32) + far[0, rows, :].astype(F32)).astype(BF16)
        return carry

    lax.fori_loop(0, 8, add_up, 0)
    near_up.start()
    far_down.wait_recv()

    def add_down(i, carry):
        here = pl.ds(pl.multiple_of(i * 32, 32), 32)
        rows = pl.ds(pl.multiple_of(256 + i * 32, 32), 32)
        part[2, rows, :] = (part[2, rows, :].astype(F32) + far[1, here, :].astype(F32)).astype(BF16)
        return carry

    lax.fori_loop(0, 8, add_down, 0)
    near_down.start()
    pair.wait_recv()

    def flatten(i, carry):
        for e in range(2):
            for h in range(2):
                block = jnp.concatenate(
                    [f5[i, e, 2 * h].astype(F32), f5[i, e, 2 * h + 1].astype(F32)], axis=0)
                factor[pl.ds(pl.multiple_of(i * 64 + 32 * e + 16 * h, 16), 16), :] = block.astype(BF16)
        return carry

    lax.fori_loop(0, 16, flatten, 0)
    invert(factor, inv, left, right, pivot)

    near_up.wait_recv()
    near_down.wait_recv()

    def total_rows(i, carry):
        rows = pl.ds(pl.multiple_of(i * 32, 32), 32)
        summed[rows, :] = (part[3, rows, :].astype(F32) + near[0, rows, :].astype(F32)
                           + near[1, rows, :].astype(F32)).astype(BF16)
        return carry

    lax.fori_loop(0, 16, total_rows, 0)

    def project(i, carry):
        cols = pl.ds(pl.multiple_of(i * 256, 256), 256)
        p = jnp.dot(summed[...], factor[:, cols], preferred_element_type=F32)
        squared[:, cols] = (p * p).astype(BF16)
        return carry

    lax.fori_loop(0, 4, project, 0)

    def moments(i, carry):
        rows = pl.ds(pl.multiple_of(i * 256, 256), 256)
        moment[rows, :] = lax.dot_general(
            summed[:, rows], squared[...], (((0,), (0,)), ((), ())), preferred_element_type=F32)
        return carry

    lax.fori_loop(0, 4, moments, 0)

    def block(i, core):
        return moment[pl.ds(pl.multiple_of((i * 2 + core) * 32, 32), 32), :].reshape(4, 8, 1024)

    def cast(i, carry):
        core_out[i] = block(i, 1 - c).astype(BF16)
        return carry

    lax.fori_loop(0, 16, cast, 0)
    across = remote(core_out, core_in, pair_send.at[1], pair_recv.at[1], m.partner)
    across.start()
    across.wait_recv()

    def add(i, carry):
        mine[i] = (block(i, c) + core_in[i].astype(F32)).astype(BF16)
        return carry

    lax.fori_loop(0, 16, add, 0)
    for d, o in enumerate(OFFSETS):
        xy, pz = m.pos[o]
        remote(mine.at[xy, pz], parts.at[d], a_send, a_recv, m.device(o)).start()
    own_rows = pl.multiple_of(((m.xy * 2 + c) * 4 + z) * 8, 8)
    total = moment[pl.ds(own_rows, 8), :] + core_in[m.xy, z].astype(F32)
    all_of(parts, a_recv).wait()
    total = lax.fori_loop(0, 63, lambda d, t: t + parts[d].astype(F32), total)
    updated = jnp.dot(total, inv[...], precision=HI, preferred_element_type=F32)

    squares = jnp.sum(updated * updated, axis=0, keepdims=True)
    for j in range(8):
        norm_out[0, j:j + 1, :] = squares[:, 128 * j:128 * j + 128]
    between = remote(norm_out.at[0], norm_in.at[63], pair_send.at[2], pair_recv.at[2], m.partner)
    between.start()
    between.wait_recv()
    norm_out[1] = norm_out[0] + norm_in[63]
    for d, o in enumerate(OFFSETS):
        remote(norm_out.at[1], norm_in.at[d], n_send, n_recv, m.device(o)).start()
    all_of(norm_in.at[pl.ds(0, 63)], n_recv).wait()
    norm = norm_out[1]
    for d in range(63):
        norm = norm + norm_in[d]
    scale = jnp.sqrt(norm * (1.0 / N) + 1e-6)
    for j in range(8):
        cols = slice(128 * j, 128 * j + 128)
        out_ref[:, cols] = updated[:, cols] / scale[j:j + 1, :]
    all_of(parts, f_send).wait()
    all_of(parts, a_send).wait()
    all_of(norm_in.at[pl.ds(0, 63)], n_send).wait()
    for copy in (pair, across, between, far_up, far_down, near_up, near_down):
        copy.wait_send()


def shards(activations, whitening, factor):
    terms = 128 * len(TERMS)
    dma = pltpu.SemaphoreType.DMA
    return pl.pallas_call(
        whole_kernel,
        out_shape=jax.ShapeDtypeStruct((8, N), F32),
        in_specs=[pl.BlockSpec(memory_space=pl.ANY)] * 2 + [pl.BlockSpec(memory_space=pltpu.VMEM)],
        out_specs=pl.BlockSpec(memory_space=pltpu.VMEM),
        scratch_shapes=[
            pltpu.VMEM((4, 512, 2048), BF16), pltpu.VMEM((2048, N), BF16), pltpu.VMEM((4, 512, N), BF16),
            pltpu.VMEM((2, 256, N), BF16), pltpu.VMEM((2, 512, N), BF16),
            pltpu.VMEM((16, 2, 4, 8, N), BF16), pltpu.VMEM((N, N), BF16), pltpu.VMEM((N, N), F32),
            pltpu.VMEM((N, terms), BF16), pltpu.VMEM((terms, N), BF16), pltpu.VMEM((128, 128), F32),
            pltpu.VMEM((512, N), BF16), pltpu.VMEM((512, N), BF16), pltpu.VMEM((N, N), F32),
            pltpu.VMEM((16, 4, 8, N), BF16), pltpu.VMEM((16, 4, 8, N), BF16), pltpu.VMEM((16, 4, 8, N), BF16),
            pltpu.VMEM((63, 8, N), BF16), pltpu.VMEM((2, 8, 128), F32), pltpu.VMEM((64, 8, 128), F32),
            dma((4,)), dma, dma, dma, dma, dma, dma, dma, dma((3,)), dma((3,)), dma((2,)), dma((2,)), dma((2,)), dma((2,))],
        compiler_params=pltpu.CompilerParams(
            collective_id=0, has_side_effects=True, vmem_limit_bytes=56 * 2**20),
    )(activations, whitening, factor)


def solution(mesh):
    placed = (P("dp", "tensor"), P("tensor", None), P(("dp", "tensor"), None))
    return jax.shard_map(
        shards, mesh=mesh, in_specs=placed, out_specs=P(("dp", "tensor"), None), check_vma=False
    )
```

time: 908 us -> 118 us (0.13)
  waiting for transfers between devices: 444 us -> 0 us
  other arithmetic: 263 us -> 0 us
  Pallas kernels: 0 us -> 116 us
  blocking collectives: 70.4 us -> 0 us
  matrix products: 68.9 us -> 0 us
  local copies, waits for them, and re-layouts: 34.8 us -> 1.38 us
  between operations: 20.4 us -> 0.01 us
    reduce_scatter x2 -> x0, waiting for transfers between devices: 365 us -> none  [the longest x1 365 us: shards(): lax.psum_scatter(lax.dot_general(summed, squared, (((0,), (0,)), ((), ())...]
    another operation x33 -> x0, other arithmetic: 256 us -> none  [the longest x30 172 us: solve_rows(): lower = jnp.linalg.cholesky(hadamard)]
    pallas_call x0 -> x1, Pallas kernels: none -> 116 us  [shards(): pl.pallas_call(whole_kernel, out_shape=jax.ShapeDtypeStruct((8, N), F32),...]
    all_gather x1 -> x0, waiting for transfers between devices: 77.6 us -> none  [shards(): whole_factor = lax.all_gather(factor, ('dp', 'tensor'), axis=0, tiled=True)]
    psum x1 -> x0, blocking collectives: 70.4 us -> none  [shards(): lax.psum(jnp.sum(updated * updated, axis=0), ('dp', 'tensor'))]
    another operation x44 -> x0, matrix products: 44.7 us -> none  [the longest x14 23.3 us: solve_rows(): lower = jnp.linalg.cholesky(hadamard)]
    another operation x37 -> x0, local copies, waits for them, and re-layouts: 24.9 us -> none
    dot_general x3 -> x0, matrix products: 24.2 us -> none  [the longest x1 13.8 us: shards(): jnp.dot(activations, whitening, preferred_element_type=jnp.float32)]
  transfers between devices with their start and end apart: 3 -> 0, of which waited for: 2 -> 0; matrix products, arithmetic and copies ran while one was open for 37% -> 0% of each run, Pallas kernels for 0% -> 0%
where the time goes in v2:
time: 118 us; the launch traced here: 117 us
  Pallas kernels  116 us (98%)
  local copies, waits for them, and re-layouts  1.38 us (1%)
    pallas_call x1, Pallas kernels, shards(): pl.pallas_call(whole_kernel, out_shape=jax.ShapeDtypeStruct((8, N), F32),...  116 us

profile of v2, /device:TPU:1, one launch (start us, length us, event | category | flops | bytes accessed | tf_op | source)
XLA Modules:
  0.0 117.5 jit_solution(10877512171027642137)
XLA Ops:
  0.0 116.1 %shard_map.37 = f32[8,1024]{1,0:T(8,128)} custom-call(bf16[2048,2048]{1,0:T(8,128)(2,1)} %act_ref.1, bf16[2048,1024]{1,0:T(8,128)(2,1)} %wh_ref.1, bf16[8,1024]{1,0:T(8,128)(2,1)} %f_ref.1), custom_call_target="tpu_custom_call" | custom-call | tf_op jit(solution)/shard_map/pallas_call | solution.py:370
  116.1 1.4 %copy.5 = f32[8,1024]{1,0:T(8,128)} copy(f32[8,1024]{1,0:T(8,128)} %shard_map.37) | data formatting | bytes 65536

commit v3 on v2

--- a/solution.py
+++ b/solution.py
@@ -101,7 +101,7 @@
     col = lax.broadcasted_iota(jnp.int32, (rows, cols), 1) + j
     return g * g + jnp.where(row == col, 0.1, 0.0)
 
-def invert(f_ref, inv_ref, left, right, pivot):
+def invert(f_ref, inv_ref, left, right, pivot, between):
     def run(todo, rate):
         def fill():
             for _ in range(rate):
@@ -154,6 +154,7 @@
         return [column] + [panel(j) for j in range(4)] + [update(r, c) for r in range(8) for c in range(2)]
 
     def step(k, carry):
+        between(k)
         k0 = pl.multiple_of(k * 128, 128)
         n0 = pl.multiple_of(k * 128 + 128, 128)
         p = pivot[...]
@@ -173,7 +174,8 @@
 
 
 MESH = pl.DeviceIdType.MESH
-OFFSETS = [(a, b, e) for a in range(4) for b in range(4) for e in range(4) if a + b + e > 0]
+PARTS = ((0, 384, (0, 1, 2)), (384, 384, (1, 2, 0)), (768, 256, (2, 0, 1)))
+STAGES = (3, 4, 5, 6, None)
 
 
 def ring(i):
@@ -183,22 +185,33 @@
 class Map:
     def __init__(self):
         dp, z = lax.axis_index("dp"), lax.axis_index("tensor")
-        x, y, self.c = dp // 8, (dp // 2) % 4, dp % 2
-        xs, ys, self.zs = ring(x), ring(y), ring(z)
-        self.pos = {o: (xs[o[0]] * 4 + ys[o[1]], self.zs[o[2]]) for o in OFFSETS}
-        self.xy, self.z = x * 4 + y, z
-        self.partner = (self.xy * 2 + 1 - self.c, z)
-
-    def device(self, o):
-        xy, z = self.pos[o]
-        return (xy * 2 + self.c, z)
+        self.c = dp % 2
+        self.at = (dp // 8, (dp // 2) % 4, z)
+        self.rings = [ring(i) for i in self.at]
+        self.partner = self.name(self.at, 1 - self.c)
+
+    def name(self, at, core):
+        return ((at[0] * 4 + at[1]) * 2 + core, at[2])
+
+    def peer(self, axis, s):
+        at = list(self.at)
+        at[axis] = self.rings[axis][s]
+        return self.name(at, self.c)
+
+    def close(self):
+        x, y, _ = self.at
+        zs = self.rings[2]
+        return [self.name((x, y, zs[s]), core) for core in (self.c, 1 - self.c) for s in range(4) if core is not self.c or s]
+
+    def plane(self):
+        xs, ys, _ = self.rings
+        return [self.name((xs[a], ys[b], self.at[2]), self.c) for a in range(4) for b in range(4) if a + b]
 
 
 def greet(m):
     barrier = pltpu.get_barrier_semaphore()
-    for o in OFFSETS:
-        pl.semaphore_signal(barrier, inc=1, device_id=m.device(o), device_id_type=MESH)
-    pl.semaphore_signal(barrier, inc=1, device_id=m.partner, device_id_type=MESH)
+    for device in m.close() + m.plane():
+        pl.semaphore_signal(barrier, inc=1, device_id=device, device_id_type=MESH)
     return barrier
 
 
@@ -213,33 +226,71 @@
 
 def whole_kernel(act_ref, wh_ref, f_ref, out_ref,
                  act, wh, part, far, near, f5, factor, inv, left, right, pivot, summed, squared, moment,
-                 core_out, core_in, mine, parts, norm_out, norm_in,
-                 act_sem, wh_sem, f_send, f_recv, a_send, a_recv, n_send, n_recv, pair_send, pair_recv, far_send, far_recv, near_send, near_recv):
+                 core_out, core_in, mine, in1, out2, in2, out3, in3, total, norm_out, norm_in,
+                 act_sem, wh_sem, f_send, f_recv, l_send, l_recv, s_send, s_recv, n_send, n_recv,
+                 pair_send, pair_recv, far_send, far_recv, near_send, near_recv):
     m = Map()
-    c, z = m.c, m.z
+    c = m.c
+    x, y, z = m.at
     barrier = greet(m)
-    order = (m.zs[2], m.zs[1], m.zs[3], z)
+    zs = m.rings[2]
+    order = (zs[2], zs[1], zs[3], z)
+
+    def load(r):
+        rows = pl.ds(pl.multiple_of(order[r] * 512, 512), 512)
+        return pltpu.make_async_copy(act_ref.at[rows, :], act.at[r], act_sem.at[r])
+
+    load_wh = pltpu.make_async_copy(wh_ref, wh, wh_sem)
+    load_wh.start()
     for r in range(4):
-        rows = pl.ds(pl.multiple_of(order[r] * 512, 512), 512)
-        pltpu.make_async_copy(act_ref.at[rows, :], act.at[r], act_sem.at[r]).start()
-        if r == 0:
-            pltpu.make_async_copy(wh_ref, wh, wh_sem).start()
-    f5[m.xy, c, z] = f_ref[...]
-    pl.semaphore_wait(barrier, 64)
-
-    home = f5.at[m.xy, c, z]
-    for o in OFFSETS:
-        remote(f_ref, home, f_send, f_recv, m.device(o)).start()
-
-    up, down = m.device((0, 0, 1)), m.device((0, 0, 3))
+        load(r).start()
+    f5[x, y, c, z] = f_ref[...]
+    pl.semaphore_wait(barrier, 22)
+
+    first, second = pl.ds(0, 512), pl.ds(512, 512)
+    hops = [
+        (f_ref, f5.at[x, y, c, z], 2, f5.at[0, 0, 0, pl.ds(0, 3)]),
+        (f5.at[x, y, c, :, :, first], f5.at[x, y, c, :, :, first], 0, f5.at[pl.ds(0, 3), 0, 0, :, :, first]),
+        (f5.at[x, y, c, :, :, second], f5.at[x, y, c, :, :, second], 1, f5.at[pl.ds(0, 3), 0, 0, :, :, first]),
+    ]
+
+    def hop_start(i):
+        src, dst, axis, _ = hops[i]
+        for s in (1, 2, 3):
+            remote(src, dst, f_send.at[i], f_recv.at[i], m.peer(axis, s)).start()
+
+    def hop_end(i, sems):
+        all_of(hops[i][3], sems.at[i]).wait()
+
+    def strip(half, s):
+        if half == 0:
+            return f5.at[:, m.rings[1][s], c, :, :, first]
+        return f5.at[x, :, c, :, :, second] if s == 0 else f5.at[m.rings[0][s], :, c, :, :, second]
+
+    def last_hop(half, s):
+        return remote(strip(half, 0), strip(half, 0), l_send.at[half, s - 1], l_recv.at[half, s - 1], m.peer(1 - half, s))
+
+    def pair(half, s):
+        return remote(strip(half, s), strip(half, s), pair_send.at[0], pair_recv.at[0], m.partner)
+
+    hop_start(0)
+
+    up, down = m.peer(2, 1), m.peer(2, 3)
     far_up = remote(part.at[0, pl.ds(0, 256)], far.at[0], far_send.at[0], far_recv.at[0], up)
     far_down = remote(part.at[0, pl.ds(256, 256)], far.at[1], far_send.at[1], far_recv.at[1], down)
-    near_up = remote(part.at[1], near.at[0], near_send.at[0], near_recv.at[0], up)
-    near_down = remote(part.at[2], near.at[1], near_send.at[1], near_recv.at[1], down)
-    pltpu.make_async_copy(wh_ref, wh, wh_sem).wait()
+
+    def near_copy(slot, half):
+        rows = pl.ds(256 * half, 256)
+        return remote(part.at[1 + slot, rows], near.at[slot, rows], near_send.at[slot, half], near_recv.at[slot, half],
+                      down if slot else up)
+
+    load_wh.wait()
     for r in range(4):
-        rows = pl.ds(pl.multiple_of(order[r] * 512, 512), 512)
-        pltpu.make_async_copy(act_ref.at[rows, :], act.at[r], act_sem.at[r]).wait()
+        load(r).wait()
+        if r == 0:
+            hop_end(0, f_recv)
+            hop_start(1)
+            hop_start(2)
 
         def tile(i, carry, r=r):
             cols = pl.ds(pl.multiple_of(i * 256, 256), 256)
@@ -250,117 +301,229 @@
         if r == 0:
             far_up.start()
             far_down.start()
-
-    all_of(parts, f_recv).wait()
-    pair = remote(f5.at[:, c], f5.at[:, c], pair_send.at[0], pair_recv.at[0], m.partner)
-    pair.start()
-
-    far_up.wait_recv()
-
-    def add_up(i, carry):
-        rows = pl.ds(pl.multiple_of(i * 32, 32), 32)
-        part[1, rows, :] = (part[1, rows, :].astype(F32) + far[0, rows, :].astype(F32)).astype(BF16)
-        return carry
-
-    lax.fori_loop(0, 8, add_up, 0)
-    near_up.start()
-    far_down.wait_recv()
-
-    def add_down(i, carry):
-        here = pl.ds(pl.multiple_of(i * 32, 32), 32)
-        rows = pl.ds(pl.multiple_of(256 + i * 32, 32), 32)
-        part[2, rows, :] = (part[2, rows, :].astype(F32) + far[1, here, :].astype(F32)).astype(BF16)
-        return carry
-
-    lax.fori_loop(0, 8, add_down, 0)
-    near_down.start()
-    pair.wait_recv()
+            hop_end(1, f_recv)
+            hop_end(2, f_recv)
+            for s in (1, 2, 3):
+                for half in (0, 1):
+                    last_hop(half, s).start()
+            for half in (0, 1):
+                pair(half, 0).start()
+        if r == 1:
+            near_copy(0, 1).start()
+        if r == 2:
+            near_copy(1, 0).start()
+            for s in (1, 3, 2):
+                for half in (0, 1):
+                    last_hop(half, s).wait_recv()
+                    pair(half, 4 - s).start()
+
+    def forward(copy_in, slot):
+        begin = 256 * slot
+        copy_in.wait_recv()
+
+        def add(i, carry):
+            here = pl.ds(pl.multiple_of(i * 32, 32), 32)
+            rows = pl.ds(pl.multiple_of(begin + i * 32, 32), 32)
+            part[1 + slot, rows, :] = (part[1 + slot, rows, :].astype(F32) + far[slot, here, :].astype(F32)).astype(BF16)
+            return carry
+
+        lax.fori_loop(0, 8, add, 0)
+        near_copy(slot, slot).start()
+
+    forward(far_up, 0)
+    forward(far_down, 1)
+    all_of(f5.at[:, :, 0], pair_recv.at[0]).wait()
 
     def flatten(i, carry):
         for e in range(2):
             for h in range(2):
                 block = jnp.concatenate(
-                    [f5[i, e, 2 * h].astype(F32), f5[i, e, 2 * h + 1].astype(F32)], axis=0)
+                    [f5[i // 4, i % 4, e, 2 * h].astype(F32), f5[i // 4, i % 4, e, 2 * h + 1].astype(F32)], axis=0)
                 factor[pl.ds(pl.multiple_of(i * 64 + 32 * e + 16 * h, 16), 16), :] = block.astype(BF16)
         return carry
 
     lax.fori_loop(0, 16, flatten, 0)
-    invert(factor, inv, left, right, pivot)
-
-    near_up.wait_recv()
-    near_down.wait_recv()
-
-    def total_rows(i, carry):
-        rows = pl.ds(pl.multiple_of(i * 32, 32), 32)
-        summed[rows, :] = (part[3, rows, :].astype(F32) + near[0, rows, :].astype(F32)
-                           + near[1, rows, :].astype(F32)).astype(BF16)
-        return carry
-
-    lax.fori_loop(0, 16, total_rows, 0)
-
-    def project(i, carry):
-        cols = pl.ds(pl.multiple_of(i * 256, 256), 256)
-        p = jnp.dot(summed[...], factor[:, cols], preferred_element_type=F32)
-        squared[:, cols] = (p * p).astype(BF16)
-        return carry
-
-    lax.fori_loop(0, 4, project, 0)
-
-    def moments(i, carry):
-        rows = pl.ds(pl.multiple_of(i * 256, 256), 256)
-        moment[rows, :] = lax.dot_general(
-            summed[:, rows], squared[...], (((0,), (0,)), ((), ())), preferred_element_type=F32)
-        return carry
-
-    lax.fori_loop(0, 4, moments, 0)
-
-    def block(i, core):
-        return moment[pl.ds(pl.multiple_of((i * 2 + core) * 32, 32), 32), :].reshape(4, 8, 1024)
-
-    def cast(i, carry):
-        core_out[i] = block(i, 1 - c).astype(BF16)
-        return carry
-
-    lax.fori_loop(0, 16, cast, 0)
+
     across = remote(core_out, core_in, pair_send.at[1], pair_recv.at[1], m.partner)
-    across.start()
-    across.wait_recv()
-
-    def add(i, carry):
-        mine[i] = (block(i, c) + core_in[i].astype(F32)).astype(BF16)
-        return carry
-
-    lax.fori_loop(0, 16, add, 0)
-    for d, o in enumerate(OFFSETS):
-        xy, pz = m.pos[o]
-        remote(mine.at[xy, pz], parts.at[d], a_send, a_recv, m.device(o)).start()
-    own_rows = pl.multiple_of(((m.xy * 2 + c) * 4 + z) * 8, 8)
-    total = moment[pl.ds(own_rows, 8), :] + core_in[m.xy, z].astype(F32)
-    all_of(parts, a_recv).wait()
-    total = lax.fori_loop(0, 63, lambda d, t: t + parts[d].astype(F32), total)
-    updated = jnp.dot(total, inv[...], precision=HI, preferred_element_type=F32)
+
+    def rows_of(i, core):
+        return pl.ds(pl.multiple_of((i * 2 + core) * 32, 32), 32)
+
+    def stage_moment():
+        for slot in (0, 1):
+            for half in (0, 1):
+                near_copy(slot, half).wait_recv()
+
+        def add(i, carry):
+            rows = pl.ds(pl.multiple_of(i * 32, 32), 32)
+            summed[rows, :] = (part[3, rows, :].astype(F32) + near[0, rows, :].astype(F32)
+                               + near[1, rows, :].astype(F32)).astype(BF16)
+            return carry
+
+        lax.fori_loop(0, 16, add, 0)
+
+        def project(i, carry):
+            cols = pl.ds(pl.multiple_of(i * 256, 256), 256)
+            p = jnp.dot(summed[...], factor[:, cols], preferred_element_type=F32)
+            squared[:, cols] = (p * p).astype(BF16)
+            return carry
+
+        lax.fori_loop(0, 4, project, 0)
+
+        def moments(i, carry):
+            rows = pl.ds(pl.multiple_of(i * 256, 256), 256)
+            moment[rows, :] = lax.dot_general(
+                summed[:, rows], squared[...], (((0,), (0,)), ((), ())), preferred_element_type=F32)
+            return carry
+
+        lax.fori_loop(0, 4, moments, 0)
+
+        def cast(i, carry):
+            core_out[i] = moment[rows_of(i, 1 - c), :].reshape(4, 8, N).astype(BF16)
+            return carry
+
+        lax.fori_loop(0, 16, cast, 0)
+        across.start()
+
+    def pick(ref, fixed, cols):
+        index = [fixed.get(axis, slice(None)) for axis in range(3)]
+        return ref.at[(*index, slice(None), pl.ds(cols[0], cols[1]))]
+
+    def send1(p, s):
+        lo, width, (a, b, e) = PARTS[p]
+        src = pick(mine, {a: m.rings[a][s]}, (lo, width))
+        return remote(src, in1.at[s - 1, :, :, :, pl.ds(lo, width)], s_send.at[0, p], s_recv.at[0, p], m.peer(a, s))
+
+    def send2(p, s):
+        lo, width, (a, b, e) = PARTS[p]
+        src = out2.at[m.rings[b][s], :, :, pl.ds(lo, width)]
+        return remote(src, in2.at[s - 1, :, :, pl.ds(lo, width)], s_send.at[1, p], s_recv.at[1, p], m.peer(b, s))
+
+    def send3(p, s):
+        lo, width, (a, b, e) = PARTS[p]
+        src = out3.at[m.rings[e][s], :, pl.ds(lo, width)]
+        return remote(src, in3.at[s - 1, :, pl.ds(lo, width)], s_send.at[2, p], s_recv.at[2, p], m.peer(e, s))
+
+    def landed(level, p, sems):
+        lo, width, _ = PARTS[p]
+        ref = (in1.at[:, :, :, :, pl.ds(lo, width)], in2.at[:, :, :, pl.ds(lo, width)], in3.at[:, :, pl.ds(lo, width)])[level]
+        all_of(ref, sems.at[level, p]).wait()
+
+    def stage_cores():
+        across.wait_recv()
+
+        def add(i, carry):
+            block = moment[rows_of(i, c), :].reshape(4, 8, N) + core_in[i].astype(F32)
+            moment[rows_of(i, c), :] = block.reshape(32, N)
+            mine[i // 4, i % 4] = block.astype(BF16)
+            return carry
+
+        lax.fori_loop(0, 16, add, 0)
+        for s in (1, 2, 3):
+            for p in range(3):
+                send1(p, s).start()
+
+    def stage_one():
+        for p in range(3):
+            lo, width, (a, b, e) = PARTS[p]
+            cols = pl.ds(lo, width)
+            landed(0, p, s_recv)
+
+            def add(i, carry):
+                ib, ie = i // 4, i % 4
+                index = [None] * 3
+                index[a], index[b], index[e] = m.at[a], ib, ie
+                row = pl.multiple_of((((index[0] * 4 + index[1]) * 2 + c) * 4 + index[2]) * 8, 8)
+                j, k = (ib, ie) if b < e else (ie, ib)
+                t = moment[pl.ds(row, 8), cols]
+                for s in range(3):
+                    t = t + in1[s, j, k, :, cols].astype(F32)
+                moment[pl.ds(row, 8), cols] = t
+                out2[ib, ie, :, cols] = t.astype(BF16)
+                return carry
+
+            lax.fori_loop(0, 16, add, 0)
+            for s in (1, 2, 3):
+                send2(p, s).start()
+
+    def stage_two():
+        for p in range(3):
+            lo, width, (a, b, e) = PARTS[p]
+            cols = pl.ds(lo, width)
+            landed(1, p, s_recv)
+
+            def add(ie, carry):
+                index = list(m.at)
+                index[e] = ie
+                row = pl.multiple_of((((index[0] * 4 + index[1]) * 2 + c) * 4 + index[2]) * 8, 8)
+                t = moment[pl.ds(row, 8), cols]
+                for s in range(3):
+                    t = t + in2[s, ie, :, cols].astype(F32)
+                moment[pl.ds(row, 8), cols] = t
+                out3[ie, :, cols] = t.astype(BF16)
+                return carry
+
+            lax.fori_loop(0, 4, add, 0)
+            for s in (1, 2, 3):
+                send3(p, s).start()
+
+    def stage_three():
+        own = pl.multiple_of((((x * 4 + y) * 2 + c) * 4 + z) * 8, 8)
+        for p in range(3):
+            lo, width, _ = PARTS[p]
+            cols = pl.ds(lo, width)
+            landed(2, p, s_recv)
+            t = moment[pl.ds(own, 8), cols]
+            for s in range(3):
+                t = t + in3[s, :, cols].astype(F32)
+            total[:, cols] = t
+
+    stages = (stage_moment, stage_cores, stage_one, stage_two, stage_three)
+
+    def between(k):
+        for stage, when in zip(stages, STAGES):
+            if when is not None:
+                pl.when(k == when)(stage)
+
+    invert(factor, inv, left, right, pivot, between)
+    for stage, when in zip(stages, STAGES):
+        if when is None:
+            stage()
+    updated = jnp.dot(total[...], inv[...], precision=HI, preferred_element_type=F32)
 
     squares = jnp.sum(updated * updated, axis=0, keepdims=True)
     for j in range(8):
         norm_out[0, j:j + 1, :] = squares[:, 128 * j:128 * j + 128]
-    between = remote(norm_out.at[0], norm_in.at[63], pair_send.at[2], pair_recv.at[2], m.partner)
-    between.start()
-    between.wait_recv()
-    norm_out[1] = norm_out[0] + norm_in[63]
-    for d, o in enumerate(OFFSETS):
-        remote(norm_out.at[1], norm_in.at[d], n_send, n_recv, m.device(o)).start()
-    all_of(norm_in.at[pl.ds(0, 63)], n_recv).wait()
-    norm = norm_out[1]
-    for d in range(63):
-        norm = norm + norm_in[d]
+    close, plane = m.close(), m.plane()
+    for i, device in enumerate(close):
+        remote(norm_out.at[0], norm_in.at[i], n_send.at[0], n_recv.at[0], device).start()
+    all_of(norm_in.at[pl.ds(0, 7)], n_recv.at[0]).wait()
+    norm = tree([norm_out[0]] + [norm_in[i] for i in range(7)])
+    norm_out[1] = norm
+    for i, device in enumerate(plane):
+        remote(norm_out.at[1], norm_in.at[7 + i], n_send.at[1], n_recv.at[1], device).start()
+    all_of(norm_in.at[pl.ds(7, 15)], n_recv.at[1]).wait()
+    norm = tree([norm] + [norm_in[7 + i] for i in range(15)])
     scale = jnp.sqrt(norm * (1.0 / N) + 1e-6)
     for j in range(8):
         cols = slice(128 * j, 128 * j + 128)
         out_ref[:, cols] = updated[:, cols] / scale[j:j + 1, :]
-    all_of(parts, f_send).wait()
-    all_of(parts, a_send).wait()
-    all_of(norm_in.at[pl.ds(0, 63)], n_send).wait()
-    for copy in (pair, across, between, far_up, far_down, near_up, near_down):
+
+    for i in range(3):
+        hop_end(i, f_send)
+    for s in (1, 2, 3):
+        for half in (0, 1):
+            last_hop(half, s).wait_send()
+    for level in range(3):
+        for p in range(3):
+            landed(level, p, s_send)
+    all_of(norm_in.at[pl.ds(0, 7)], n_send.at[0]).wait()
+    all_of(norm_in.at[pl.ds(7, 15)], n_send.at[1]).wait()
+    all_of(f5.at[:, :, 0], pair_send.at[0]).wait()
+    for slot in (0, 1):
+        for half in (0, 1):
+            near_copy(slot, half).wait_send()
+    for copy in (across, far_up, far_down):
         copy.wait_send()
 
 
@@ -375,12 +538,15 @@
         scratch_shapes=[
             pltpu.VMEM((4, 512, 2048), BF16), pltpu.VMEM((2048, N), BF16), pltpu.VMEM((4, 512, N), BF16),
             pltpu.VMEM((2, 256, N), BF16), pltpu.VMEM((2, 512, N), BF16),
-            pltpu.VMEM((16, 2, 4, 8, N), BF16), pltpu.VMEM((N, N), BF16), pltpu.VMEM((N, N), F32),
+            pltpu.VMEM((4, 4, 2, 4, 8, N), BF16), pltpu.VMEM((N, N), BF16), pltpu.VMEM((N, N), F32),
             pltpu.VMEM((N, terms), BF16), pltpu.VMEM((terms, N), BF16), pltpu.VMEM((128, 128), F32),
             pltpu.VMEM((512, N), BF16), pltpu.VMEM((512, N), BF16), pltpu.VMEM((N, N), F32),
-            pltpu.VMEM((16, 4, 8, N), BF16), pltpu.VMEM((16, 4, 8, N), BF16), pltpu.VMEM((16, 4, 8, N), BF16),
-            pltpu.VMEM((63, 8, N), BF16), pltpu.VMEM((2, 8, 128), F32), pltpu.VMEM((64, 8, 128), F32),
-            dma((4,)), dma, dma, dma, dma, dma, dma, dma, dma((3,)), dma((3,)), dma((2,)), dma((2,)), dma((2,)), dma((2,))],
+            pltpu.VMEM((16, 4, 8, N), BF16), pltpu.VMEM((16, 4, 8, N), BF16), pltpu.VMEM((4, 4, 4, 8, N), BF16),
+            pltpu.VMEM((3, 4, 4, 8, N), BF16), pltpu.VMEM((4, 4, 8, N), BF16), pltpu.VMEM((3, 4, 8, N), BF16),
+            pltpu.VMEM((4, 8, N), BF16), pltpu.VMEM((3, 8, N), BF16), pltpu.VMEM((8, N), F32),
+            pltpu.VMEM((2, 8, 128), F32), pltpu.VMEM((22, 8, 128), F32),
+            dma((4,)), dma, dma((3,)), dma((3,)), dma((2, 3)), dma((2, 3)), dma((3, 3)), dma((3, 3)), dma((2,)), dma((2,)),
+            dma((2,)), dma((2,)), dma((2,)), dma((2,)), dma((2, 2)), dma((2, 2))],
         compiler_params=pltpu.CompilerParams(
             collective_id=0, has_side_effects=True, vmem_limit_bytes=56 * 2**20),
     )(activations, whitening, factor)

time: 118 us -> 90.8 us (0.77)
  Pallas kernels: 116 us -> 89.2 us
    pallas_call x1, Pallas kernels: 116 us -> 89.2 us  [shards(): pl.pallas_call(whole_kernel, out_shape=jax.ShapeDtypeStruct((8, N), F32),...]
where the time goes in v3:
time: 90.8 us; the launch traced here: 90.6 us
  Pallas kernels  89.2 us (98%)
  local copies, waits for them, and re-layouts  1.38 us (2%)
    pallas_call x1, Pallas kernels, shards(): pl.pallas_call(whole_kernel, out_shape=jax.ShapeDtypeStruct((8, N), F32),...  89.2 us

profile of v3, /device:TPU:1, one launch (start us, length us, event | category | flops | bytes accessed | tf_op | source)
XLA Modules:
  0.0 90.6 jit_solution(1536523451843483680)
XLA Ops:
  0.0 89.2 %shard_map.37 = f32[8,1024]{1,0:T(8,128)} custom-call(bf16[2048,2048]{1,0:T(8,128)(2,1)} %act_ref.1, bf16[2048,1024]{1,0:T(8,128)(2,1)} %wh_ref.1, bf16[8,1024]{1,0:T(8,128)(2,1)} %f_ref.1), custom_call_target="tpu_custom_call" | custom-call | tf_op jit(solution)/shard_map/pallas_call | solution.py:533
  89.2 1.4 %copy.5 = f32[8,1024]{1,0:T(8,128)} copy(f32[8,1024]{1,0:T(8,128)} %shard_map.37) | data formatting | bytes 65536

commit v4 on v3

--- a/solution.py
+++ b/solution.py
@@ -84,9 +84,10 @@
                 rows[i] = jnp.where(inside, 0.0, rows[i]) - u[8 * n:8 * n + 8]
     return rows
 
-TERMS = ((0, 0), (0, 1), (1, 0), (0, 2), (1, 1), (2, 0))
+TERMS = ((0, 0), (0, 1), (1, 0), (1, 1))
 SIZE = 64
 N = 1024
+LAST = N - 128
 
 def split(x):
     one = x.astype(BF16)
@@ -169,8 +170,6 @@
         return carry
 
     lax.fori_loop(0, N // 128 - 1, step, 0)
-    for go in work(N - 128):
-        go()
 
 
 MESH = pl.DeviceIdType.MESH
@@ -297,10 +296,20 @@
             part[r, :, cols] = jnp.dot(act[r], wh[:, cols], preferred_element_type=F32).astype(BF16)
             return carry
 
-        lax.fori_loop(0, 4, tile, 0)
+        def half_tile(i, carry, r=r):
+            rows = pl.ds(pl.multiple_of((i // 4) * 256, 256), 256)
+            cols = pl.ds(pl.multiple_of((i % 4) * 256, 256), 256)
+            part[r, rows, cols] = jnp.dot(act[r, rows, :], wh[:, cols], preferred_element_type=F32).astype(BF16)
+            return carry
+
         if r == 0:
+            lax.fori_loop(0, 4, half_tile, 0)
             far_up.start()
+            lax.fori_loop(4, 8, half_tile, 0)
             far_down.start()
+        else:
+            lax.fori_loop(0, 4, tile, 0)
+        if r == 0:
             hop_end(1, f_recv)
             hop_end(2, f_recv)
             for s in (1, 2, 3):
@@ -423,47 +432,62 @@
             for p in range(3):
                 send1(p, s).start()
 
+    def gather_sum(row, many, cols, blocks):
+        rows = pl.ds(pl.multiple_of(row, 8), 8 * many)
+        t = moment[rows, cols]
+        for block in blocks:
+            t = t + block.astype(F32).reshape(8 * many, cols.size)
+        moment[rows, cols] = t
+        return t.astype(BF16).reshape(many, 8, cols.size)
+
+    def row_at(ix, iy, iz):
+        return (((ix * 4 + iy) * 2 + c) * 4 + iz) * 8
+
     def stage_one():
-        for p in range(3):
-            lo, width, (a, b, e) = PARTS[p]
-            cols = pl.ds(lo, width)
-            landed(0, p, s_recv)
-
-            def add(i, carry):
-                ib, ie = i // 4, i % 4
-                index = [None] * 3
-                index[a], index[b], index[e] = m.at[a], ib, ie
-                row = pl.multiple_of((((index[0] * 4 + index[1]) * 2 + c) * 4 + index[2]) * 8, 8)
-                j, k = (ib, ie) if b < e else (ie, ib)
-                t = moment[pl.ds(row, 8), cols]
-                for s in range(3):
-                    t = t + in1[s, j, k, :, cols].astype(F32)
-                moment[pl.ds(row, 8), cols] = t
-                out2[ib, ie, :, cols] = t.astype(BF16)
-                return carry
-
-            lax.fori_loop(0, 16, add, 0)
-            for s in (1, 2, 3):
-                send2(p, s).start()
+        spans = [pl.ds(lo, width) for lo, width, _ in PARTS]
+        landed(0, 0, s_recv)
+
+        def add_x(i, carry):
+            out2[i, :, :, spans[0]] = gather_sum(
+                row_at(x, i, 0), 4, spans[0], [in1[s, i, :, :, spans[0]] for s in range(3)])
+            return carry
+
+        lax.fori_loop(0, 4, add_x, 0)
+        for s in (1, 2, 3):
+            send2(0, s).start()
+        landed(0, 1, s_recv)
+
+        def add_y(i, carry):
+            out2[:, i, :, spans[1]] = gather_sum(
+                row_at(i, y, 0), 4, spans[1], [in1[s, i, :, :, spans[1]] for s in range(3)])
+            return carry
+
+        lax.fori_loop(0, 4, add_y, 0)
+        for s in (1, 2, 3):
+            send2(1, s).start()
+        landed(0, 2, s_recv)
+
+        def add_z(i, carry):
+            for j in range(4):
+                out2[i, pl.ds(j, 1), :, spans[2]] = gather_sum(
+                    row_at(i, j, z), 1, spans[2], [in1[s, i, j, :, spans[2]] for s in range(3)])
+            return carry
+
+        lax.fori_loop(0, 4, add_z, 0)
+        for s in (1, 2, 3):
+            send2(2, s).start()
 
     def stage_two():
-        for p in range(3):
-            lo, width, (a, b, e) = PARTS[p]
-            cols = pl.ds(lo, width)
+        spans = [pl.ds(lo, width) for lo, width, _ in PARTS]
+        landed(1, 0, s_recv)
+        out3[:, :, spans[0]] = gather_sum(row_at(x, y, 0), 4, spans[0], [in2[s, :, :, spans[0]] for s in range(3)])
+        for s in (1, 2, 3):
+            send3(0, s).start()
+        for p in (1, 2):
             landed(1, p, s_recv)
-
-            def add(ie, carry):
-                index = list(m.at)
-                index[e] = ie
-                row = pl.multiple_of((((index[0] * 4 + index[1]) * 2 + c) * 4 + index[2]) * 8, 8)
-                t = moment[pl.ds(row, 8), cols]
-                for s in range(3):
-                    t = t + in2[s, ie, :, cols].astype(F32)
-                moment[pl.ds(row, 8), cols] = t
-                out3[ie, :, cols] = t.astype(BF16)
-                return carry
-
-            lax.fori_loop(0, 4, add, 0)
+            for i in range(4):
+                row = row_at(i, y, z) if p == 1 else row_at(x, i, z)
+                out3[pl.ds(i, 1), :, spans[p]] = gather_sum(row, 1, spans[p], [in2[s, i, :, spans[p]] for s in range(3)])
             for s in (1, 2, 3):
                 send3(p, s).start()
 
@@ -489,7 +513,11 @@
     for stage, when in zip(stages, STAGES):
         if when is None:
             stage()
-    updated = jnp.dot(total[...], inv[...], precision=HI, preferred_element_type=F32)
+    moved = jnp.where(lax.broadcasted_iota(jnp.int32, (8, N), 1) < LAST, total[...], 0.0)
+    partly = jnp.dot(moved, inv[...], precision=HI, preferred_element_type=F32)
+    corner = jnp.dot(total[:, LAST:] - partly[:, LAST:], pivot[...], precision=HI, preferred_element_type=F32)
+    others = partly[:, :LAST] + jnp.dot(corner, inv[LAST:, :LAST], precision=HI, preferred_element_type=F32)
+    updated = jnp.concatenate([others, corner], axis=1)
 
     squares = jnp.sum(updated * updated, axis=0, keepdims=True)
     for j in range(8):

time: 90.8 us -> 87.9 us (0.968)
  Pallas kernels: 89.2 us -> 86.3 us
    pallas_call x1, Pallas kernels: 89.2 us -> 86.3 us  [shards(): pl.pallas_call(whole_kernel, out_shape=jax.ShapeDtypeStruct((8, N), F32),...]
where the time goes in v4:
time: 87.9 us; the launch traced here: 87.7 us
  Pallas kernels  86.3 us (98%)
  local copies, waits for them, and re-layouts  1.38 us (2%)
    pallas_call x1, Pallas kernels, shards(): pl.pallas_call(whole_kernel, out_shape=jax.ShapeDtypeStruct((8, N), F32),...  86.3 us

profile of v4, /device:TPU:1, one launch (start us, length us, event | category | flops | bytes accessed | tf_op | source)
XLA Modules:
  0.0 87.7 jit_solution(4258931008814651063)
XLA Ops:
  0.0 86.3 %shard_map.37 = f32[8,1024]{1,0:T(8,128)} custom-call(bf16[2048,2048]{1,0:T(8,128)(2,1)} %act_ref.1, bf16[2048,1024]{1,0:T(8,128)(2,1)} %wh_ref.1, bf16[8,1024]{1,0:T(8,128)(2,1)} %f_ref.1), custom_call_target="tpu_custom_call" | custom-call | tf_op jit(solution)/shard_map/pallas_call | solution.py:561
  86.3 1.4 %copy.5 = f32[8,1024]{1,0:T(8,128)} copy(f32[8,1024]{1,0:T(8,128)} %shard_map.37) | data formatting | bytes 65536

commit v5 on v4

--- a/solution.py
+++ b/solution.py
@@ -61,6 +61,15 @@
     rows[s] = z
     return following
 
+def product(a, b):
+    a1 = a.astype(BF16)
+    a2 = (a - a1.astype(F32)).astype(BF16)
+    b1 = b.astype(BF16)
+    b2 = (b - b1.astype(F32)).astype(BF16)
+    left = jnp.concatenate([a1, a1, a2, a2], axis=1)
+    right = jnp.concatenate([b1, b2, b1, b2], axis=0)
+    return jnp.dot(left, right, preferred_element_type=F32)
+
 def invert_block(rows, size, fill):
     lane = lax.broadcasted_iota(jnp.int32, (8, 128), 1)
     sub = lax.broadcasted_iota(jnp.int32, (8, 128), 0)
@@ -78,7 +87,7 @@
         t = jnp.concatenate(zero * (each * g) + own + zero * (16 - each * g - each), axis=0)
         for o in [(g + e) % groups for e in range(1, groups)]:
             c = jnp.concatenate([jnp.where(inside, rows[i], 0.0) for i in range(each * o, each * o + each)], axis=0)
-            u = jnp.dot(c, t, precision=HI, preferred_element_type=F32)
+            u = product(c, t)
             for n in range(each):
                 i = each * o + n
                 rows[i] = jnp.where(inside, 0.0, rows[i]) - u[8 * n:8 * n + 8]
@@ -130,7 +139,7 @@
         def panel(j):
             def go():
                 cols = slice(256 * j, 256 * j + 256)
-                t = jnp.dot(p, inv_ref[pl.ds(k0, 128), cols], precision=HI, preferred_element_type=F32)
+                t = product(p, inv_ref[pl.ds(k0, 128), cols])
                 at = col + 256 * j
                 t = jnp.where((at >= k0) & (at < k0 + 128), pp, t)
                 inv_ref[pl.ds(k0, 128), cols] = t
@@ -159,9 +168,9 @@
         k0 = pl.multiple_of(k * 128, 128)
         n0 = pl.multiple_of(k * 128 + 128, 128)
         p = pivot[...]
-        tn = jnp.dot(p, inv_ref[pl.ds(k0, 128), pl.ds(n0, 128)], precision=HI, preferred_element_type=F32)
-        d = inv_ref[pl.ds(n0, 128), pl.ds(n0, 128)] - jnp.dot(
-            inv_ref[pl.ds(n0, 128), pl.ds(k0, 128)], tn, precision=HI, preferred_element_type=F32)
+        tn = product(p, inv_ref[pl.ds(k0, 128), pl.ds(n0, 128)])
+        d = inv_ref[pl.ds(n0, 128), pl.ds(n0, 128)] - product(
+            inv_ref[pl.ds(n0, 128), pl.ds(k0, 128)], tn)
         todo = work(k0)
         nxt = invert_block([d[8 * i:8 * i + 8] for i in range(16)], SIZE, run(todo, 2))
         while todo:
@@ -255,7 +264,7 @@
 
     def hop_start(i):
         src, dst, axis, _ = hops[i]
-        for s in (1, 2, 3):
+        for s in (2, 1, 3):
             remote(src, dst, f_send.at[i], f_recv.at[i], m.peer(axis, s)).start()
 
     def hop_end(i, sems):
@@ -286,10 +295,6 @@
     load_wh.wait()
     for r in range(4):
         load(r).wait()
-        if r == 0:
-            hop_end(0, f_recv)
-            hop_start(1)
-            hop_start(2)
 
         def tile(i, carry, r=r):
             cols = pl.ds(pl.multiple_of(i * 256, 256), 256)
@@ -310,17 +315,21 @@
         else:
             lax.fori_loop(0, 4, tile, 0)
         if r == 0:
+            hop_end(0, f_recv)
+            hop_start(1)
+            hop_start(2)
+        if r == 1:
             hop_end(1, f_recv)
             hop_end(2, f_recv)
-            for s in (1, 2, 3):
+            for s in (2, 1, 3):
                 for half in (0, 1):
                     last_hop(half, s).start()
             for half in (0, 1):
                 pair(half, 0).start()
-        if r == 1:
             near_copy(0, 1).start()
         if r == 2:
             near_copy(1, 0).start()
+        if r == 3:
             for s in (1, 3, 2):
                 for half in (0, 1):
                     last_hop(half, s).wait_recv()
@@ -428,7 +437,7 @@
             return carry
 
         lax.fori_loop(0, 16, add, 0)
-        for s in (1, 2, 3):
+        for s in (2, 1, 3):
             for p in range(3):
                 send1(p, s).start()
 
@@ -453,7 +462,7 @@
             return carry
 
         lax.fori_loop(0, 4, add_x, 0)
-        for s in (1, 2, 3):
+        for s in (2, 1, 3):
             send2(0, s).start()
         landed(0, 1, s_recv)
 
@@ -463,7 +472,7 @@
             return carry
 
         lax.fori_loop(0, 4, add_y, 0)
-        for s in (1, 2, 3):
+        for s in (2, 1, 3):
             send2(1, s).start()
         landed(0, 2, s_recv)
 
@@ -474,21 +483,21 @@
             return carry
 
         lax.fori_loop(0, 4, add_z, 0)
-        for s in (1, 2, 3):
+        for s in (2, 1, 3):
             send2(2, s).start()
 
     def stage_two():
         spans = [pl.ds(lo, width) for lo, width, _ in PARTS]
         landed(1, 0, s_recv)
         out3[:, :, spans[0]] = gather_sum(row_at(x, y, 0), 4, spans[0], [in2[s, :, :, spans[0]] for s in range(3)])
-        for s in (1, 2, 3):
+        for s in (2, 1, 3):
             send3(0, s).start()
         for p in (1, 2):
             landed(1, p, s_recv)
             for i in range(4):
                 row = row_at(i, y, z) if p == 1 else row_at(x, i, z)
                 out3[pl.ds(i, 1), :, spans[p]] = gather_sum(row, 1, spans[p], [in2[s, i, :, spans[p]] for s in range(3)])
-            for s in (1, 2, 3):
+            for s in (2, 1, 3):
                 send3(p, s).start()
 
     def stage_three():
@@ -514,7 +523,11 @@
         if when is None:
             stage()
     moved = jnp.where(lax.broadcasted_iota(jnp.int32, (8, N), 1) < LAST, total[...], 0.0)
-    partly = jnp.dot(moved, inv[...], precision=HI, preferred_element_type=F32)
+    stacked = jnp.concatenate([piece.astype(F32) for piece in split(moved)], axis=0).astype(BF16)
+    partly = jnp.zeros((8, N), F32)
+    for piece in split(inv[...])[:2]:
+        products = jnp.dot(stacked, piece, preferred_element_type=F32)
+        partly = partly + ((products[16:24] + products[8:16]) + products[0:8])
     corner = jnp.dot(total[:, LAST:] - partly[:, LAST:], pivot[...], precision=HI, preferred_element_type=F32)
     others = partly[:, :LAST] + jnp.dot(corner, inv[LAST:, :LAST], precision=HI, preferred_element_type=F32)
     updated = jnp.concatenate([others, corner], axis=1)
@@ -539,7 +552,7 @@
 
     for i in range(3):
         hop_end(i, f_send)
-    for s in (1, 2, 3):
+    for s in (2, 1, 3):
         for half in (0, 1):
             last_hop(half, s).wait_send()
     for level in range(3):

time: 87.9 us -> 87 us (0.990)
  Pallas kernels: 86.3 us -> 85.4 us
    pallas_call x1, Pallas kernels: 86.3 us -> 85.4 us  [shards(): pl.pallas_call(whole_kernel, out_shape=jax.ShapeDtypeStruct((8, N), F32),...]
where the time goes in v5:
time: 87 us; the launch traced here: 86.8 us
  Pallas kernels  85.4 us (98%)
  local copies, waits for them, and re-layouts  1.38 us (2%)
    pallas_call x1, Pallas kernels, shards(): pl.pallas_call(whole_kernel, out_shape=jax.ShapeDtypeStruct((8, N), F32),...  85.4 us

profile of v5, /device:TPU:1, one launch (start us, length us, event | category | flops | bytes accessed | tf_op | source)
XLA Modules:
  0.0 86.8 jit_solution(719786625540893576)
XLA Ops:
  0.0 85.4 %shard_map.37 = f32[8,1024]{1,0:T(8,128)} custom-call(bf16[2048,2048]{1,0:T(8,128)(2,1)} %act_ref.1, bf16[2048,1024]{1,0:T(8,128)(2,1)} %wh_ref.1, bf16[8,1024]{1,0:T(8,128)(2,1)} %f_ref.1), custom_call_target="tpu_custom_call" | custom-call | tf_op jit(solution)/shard_map/pallas_call | solution.py:574
  85.4 1.4 %copy.5 = f32[8,1024]{1,0:T(8,128)} copy(f32[8,1024]{1,0:T(8,128)} %shard_map.37) | data formatting | bytes 65536

commit v6 on v5

--- a/solution.py
+++ b/solution.py
@@ -381,12 +381,12 @@
         lax.fori_loop(0, 16, add, 0)
 
         def project(i, carry):
-            cols = pl.ds(pl.multiple_of(i * 256, 256), 256)
+            cols = pl.ds(pl.multiple_of(i * 512, 512), 512)
             p = jnp.dot(summed[...], factor[:, cols], preferred_element_type=F32)
             squared[:, cols] = (p * p).astype(BF16)
             return carry
 
-        lax.fori_loop(0, 4, project, 0)
+        lax.fori_loop(0, 2, project, 0)
 
         def moments(i, carry):
             rows = pl.ds(pl.multiple_of(i * 256, 256), 256)

time: 87 us -> 86.6 us (level)
  no operation moved by 1% of the time
where the time goes in v6:
time: 86.6 us; the launch traced here: 86.4 us
  Pallas kernels  85 us (98%)
  local copies, waits for them, and re-layouts  1.38 us (2%)
    pallas_call x1, Pallas kernels, shards(): pl.pallas_call(whole_kernel, out_shape=jax.ShapeDtypeStruct((8, N), F32),...  85 us

profile of v6, /device:TPU:1, one launch (start us, length us, event | category | flops | bytes accessed | tf_op | source)
XLA Modules:
  0.0 86.4 jit_solution(6110003753898187724)
XLA Ops:
  0.0 85.0 %shard_map.37 = f32[8,1024]{1,0:T(8,128)} custom-call(bf16[2048,2048]{1,0:T(8,128)(2,1)} %act_ref.1, bf16[2048,1024]{1,0:T(8,128)(2,1)} %wh_ref.1, bf16[8,1024]{1,0:T(8,128)(2,1)} %f_ref.1), custom_call_target="tpu_custom_call" | custom-call | tf_op jit(solution)/shard_map/pallas_call | solution.py:574
  85.0 1.4 %copy.5 = f32[8,1024]{1,0:T(8,128)} copy(f32[8,1024]{1,0:T(8,128)} %shard_map.37) | data formatting | bytes 65536
